TPU v7x, 512 devices: a whole 4x4x16 slice. The times are simulated.
512 devices in a mesh: shot: 4 (over x_lo, core), slab: 128 (over z, y, x_hi).
Axes of the slice: x: 4 (x_hi: 2, x_lo: 2; x = x_hi * 2 + x_lo), y: 4, z: 16, core: 2. Of those that a mesh axis runs over, the one named last changes fastest.
Arguments:
- lame_lambda: float32 [256, 32, 128], P('slab'), may hold values from 0.5 to 1.5
- lame_mu: float32 [256, 32, 128], P('slab'), may hold values from 0.3 to 0.8
- buoyancy: float32 [256, 32, 128], P('slab'), may hold values from 0.5 to 1
- forward_state: float32 [4, 9, 256, 32, 128], P('shot', None, 'slab'), may hold values from -6 to 6
- adjoint_state: float32 [4, 9, 256, 32, 128], P('shot', None, 'slab'), may hold values from -6 to 6
- source_wavelet: float32 [4, 8], P('shot'), may hold values from -20 to 20
- source_cell: int32 [4], P('shot'), may hold values from 0 to 1048575
- residual_traces: float32 [4, 8, 16384], P('shot', None, 'slab'), may hold values from -12 to 12
- receiver_slab: int32 [16384, 1], P('slab'), may hold values from 0 to 127; in each aligned block of 128 rows (0 to 127, 128 to 255, ...) at most 2 rows name the same one
- receiver_cell: int32 [16384], P('slab'), may hold values from 0 to 8191
Outputs:
- adjoint_start: float32 [4, 9, 256, 32, 128], P('shot', None, 'slab')
- lambda_gradient: float32 [256, 32, 128], P('slab', 'shot')
- mu_gradient: float32 [256, 32, 128], P('slab', 'shot')
Inputs may be any that keep to these rules, and one draw needn't show every extreme that they name: `receiver_slab`: among the 128 receivers held by one index of slab, at most 2 lie in any one slab.
All inputs are finite; a program needn't handle non-finite values.
Results may differ from a plain program's by a relative error of at most 0.000067.
Values sent between devices are 32-bit elements; how exact they have to be, the bound alone decides.
No kernel may reach another device: no remote copies, remote signals or barrier semaphores. Data moves between devices by JAX's collectives and lax.ppermute only.
A program may use at most 64 MiB of HBM per device.

v0:
```python
import jax
import jax.numpy as jnp
from jax import lax
from jax.sharding import PartitionSpec as P

TIME_STEP = 0.3


def from_behind(value, axis, steps):
    count = lax.axis_size(axis)
    initial, last = (max(0, -steps), min(count, count - steps))
    return lax.ppermute(value, axis, [(source, source + steps) for source in range(initial, last)])


def next_cell(values, along):
    extent = values.shape[along]
    remainder = lax.slice_in_dim(values, 1, extent, axis=along)
    border = jnp.zeros_like(lax.slice_in_dim(values, 0, 1, axis=along))
    return jnp.concatenate([remainder, border], axis=along)


def prev_cell(values, along):
    extent = values.shape[along]
    remainder = lax.slice_in_dim(values, 0, extent - 1, axis=along)
    border = jnp.zeros_like(lax.slice_in_dim(values, 0, 1, axis=along))
    return jnp.concatenate([border, remainder], axis=along)


def velocity_update(velocity, stress, buoyancy, normal_after, shear_before):
    sigma_xx = stress[:, 0]
    sigma_yy = stress[:, 1]
    sigma_zz = stress[:, 2]
    sigma_xy = stress[:, 3]
    sigma_xz = stress[:, 4]
    sigma_yz = stress[:, 5]
    accel_x = (
        normal_after
        - sigma_xx
        + (sigma_xy - prev_cell(sigma_xy, 2))
        + (sigma_xz - prev_cell(sigma_xz, 3))
    )
    accel_y = (
        sigma_xy
        - shear_before[:, 0]
        + (next_cell(sigma_yy, 2) - sigma_yy)
        + (sigma_yz - prev_cell(sigma_yz, 3))
    )
    accel_z = (
        sigma_xz
        - shear_before[:, 1]
        + (sigma_yz - prev_cell(sigma_yz, 2))
        + (next_cell(sigma_zz, 3) - sigma_zz)
    )
    factor = TIME_STEP * buoyancy
    return jnp.stack(
        [
            velocity[:, 0] - factor * accel_x,
            velocity[:, 1] - factor * accel_y,
            velocity[:, 2] - factor * accel_z,
        ],
        axis=1,
    )


def stress_update(velocity, stress, lame_lambda, lame_mu, speed_before, speeds_after):
    speed_x = velocity[:, 0]
    speed_y = velocity[:, 1]
    speed_z = velocity[:, 2]
    strain_xx = speed_x - speed_before[:, 0]
    strain_yy = speed_y - prev_cell(speed_y, 2)
    strain_zz = speed_z - prev_cell(speed_z, 3)
    strain_xy = next_cell(speed_x, 2) - speed_x + (speeds_after[:, 0] - speed_y)
    strain_xz = next_cell(speed_x, 3) - speed_x + (speeds_after[:, 1] - speed_z)
    strain_yz = next_cell(speed_y, 3) - speed_y + (next_cell(speed_z, 2) - speed_z)
    dilation = strain_xx + strain_yy + strain_zz
    volume_term = lame_lambda * dilation
    twice_mu = 2.0 * lame_mu
    updated = jnp.stack(
        [
            stress[:, 0] - TIME_STEP * (volume_term + twice_mu * strain_xx),
            stress[:, 1] - TIME_STEP * (volume_term + twice_mu * strain_yy),
            stress[:, 2] - TIME_STEP * (volume_term + twice_mu * strain_zz),
            stress[:, 3] - TIME_STEP * (lame_mu * strain_xy),
            stress[:, 4] - TIME_STEP * (lame_mu * strain_xz),
            stress[:, 5] - TIME_STEP * (lame_mu * strain_yz),
        ],
        axis=1,
    )
    return (updated, (strain_xx, strain_yy, strain_zz, strain_xy, strain_xz, strain_yz))


def imaging(strains):
    strain_xx, strain_yy, strain_zz, strain_xy, strain_xz, strain_yz = strains
    dilation = strain_xx + strain_yy + strain_zz
    lambda_term = TIME_STEP * (dilation[0] * dilation[1])
    shear_term = 2.0 * (
        strain_xx[0] * strain_xx[1] + strain_yy[0] * strain_yy[1] + strain_zz[0] * strain_zz[1]
    )
    shear_term = (
        shear_term
        + strain_xy[0] * strain_xy[1]
        + strain_xz[0] * strain_xz[1]
        + strain_yz[0] * strain_yz[1]
    )
    return (lambda_term, TIME_STEP * shear_term)


def shards(
    lame_lambda,
    lame_mu,
    buoyancy,
    forward_state,
    adjoint_state,
    source_wavelet,
    source_cell,
    residual_traces,
    receiver_slab,
    receiver_cell,
):
    planes, rows_y, depth = lame_lambda.shape
    cell_count = planes * rows_y * depth
    steps_total = source_wavelet.shape[1]
    my_slab = lax.axis_index("slab")
    traces = residual_traces[0]
    target_slab = receiver_slab[:, 0]
    targets = (target_slab * cell_count + receiver_cell).astype(jnp.float32)[None, :]
    arrived, landing = (
        lax.all_gather(traces, "slab", axis=1, tiled=True),
        lax.all_gather(targets, "slab", axis=1, tiled=True),
    )
    local_cell = landing[0].astype(jnp.int32) - my_slab * cell_count
    usable = (local_cell >= 0) & (local_cell < cell_count)
    cell_index = jnp.where(usable, local_cell, 0)
    amounts = jnp.where(usable[None, :], arrived, 0.0)
    receiver_push = jnp.zeros((steps_total, cell_count), jnp.float32).at[:, cell_index].add(amounts)
    receiver_push = receiver_push.reshape(steps_total, planes, rows_y, depth)
    source_local = source_cell[0] - my_slab * cell_count
    source_spot = (
        (jnp.arange(cell_count, dtype=jnp.int32) == source_local)
        .astype(jnp.float32)
        .reshape(planes, rows_y, depth)
    )
    wavefields = jnp.concatenate([forward_state, adjoint_state], axis=0)
    grad_lambda = jnp.zeros((planes, rows_y, depth), jnp.float32)
    grad_shear = jnp.zeros((planes, rows_y, depth), jnp.float32)
    for step_index in range(steps_total):
        stress_now = wavefields[:, 3:9]
        normal_next = from_behind(stress_now[:, 0, 0:1], "slab", -1)
        shear_prev = from_behind(stress_now[:, 3:5, planes - 1 : planes], "slab", 1)
        normal_after = jnp.concatenate([stress_now[:, 0, 1:], normal_next], axis=1)
        shear_before = jnp.concatenate([shear_prev, stress_now[:, 3:5, : planes - 1]], axis=2)
        velocity = velocity_update(
            wavefields[:, 0:3], stress_now, buoyancy, normal_after, shear_before
        )
        speed_prev = from_behind(velocity[:, 0:1, planes - 1 : planes], "slab", 1)
        speed_next = from_behind(velocity[:, 1:3, 0:1], "slab", -1)
        speed_before = jnp.concatenate([speed_prev, velocity[:, 0:1, : planes - 1]], axis=2)
        speeds_after = jnp.concatenate([velocity[:, 1:3, 1:], speed_next], axis=2)
        stress, strains = stress_update(
            velocity, stress_now, lame_lambda, lame_mu, speed_before, speeds_after
        )
        lambda_term, shear_term = imaging(strains)
        grad_lambda = grad_lambda + lambda_term
        grad_shear = grad_shear + shear_term
        pushes = jnp.stack([source_spot * source_wavelet[0, step_index], receiver_push[step_index]])
        stress = stress.at[:, 0:3].add(-TIME_STEP * pushes[:, None])
        wavefields = jnp.concatenate([velocity, stress], axis=1)
    lambda_part, shear_part = (
        lax.psum_scatter(grad_lambda, "shot", scatter_dimension=1, tiled=True),
        lax.psum_scatter(grad_shear, "shot", scatter_dimension=1, tiled=True),
    )
    return (wavefields[1:2], lambda_part, shear_part)


def solution(mesh):
    in_specs = (
        P("slab", None, None),
        P("slab", None, None),
        P("slab", None, None),
        P("shot", None, "slab", None, None),
        P("shot", None, "slab", None, None),
        P("shot", None),
        P("shot"),
        P("shot", None, "slab"),
        P("slab", None),
        P("slab"),
    )
    out_specs = (
        P("shot", None, "slab", None, None),
        P("slab", "shot", None),
        P("slab", "shot", None),
    )
    return jax.shard_map(shards, mesh=mesh, in_specs=in_specs, out_specs=out_specs, check_vma=False)
```

profile of v0, /device:TPU:1, one launch (start us, length us, event | category | flops | bytes accessed | tf_op | source)
XLA Modules:
  0.0 1154.6 jit_solution(3995360313206360715)
XLA Ops:
  8.0 5.5 collective-permute-start.2
  21.1 304.9 %all-gather.2 = f32[128,1,128]{2,1,0:T(1,128)S(1)} all-gather(f32[1,1,128]{2,1,0:T(1,128)S(1)} %fusion.300), channel_id=2, replica_groups=mesh['shot'=4,'slab'=128] {'slab'}, dimensions={0}, use_global_device_ids=true | all-gather | bytes 66048 | tf_op jit(solution)/shard_map/all_gather | solution.py:129
  326.0 294.9 %all-gather.1 = f32[1,8,16384]{2,1,0:T(8,128)S(1)} all-gather(f32[1,8,128]{2,1,0:T(8,128)} %param.33), channel_id=3, replica_groups=mesh['shot'=4,'slab'=128] {'slab'}, dimensions={2}, use_global_device_ids=true | all-gather | bytes 528384 | tf_op jit(solution)/shard_map/all_gather | solution.py:128
  620.9 5.3 copy.267
  626.3 115.1 %scatter_custom_fusion = f32[8,8192]{0,1:T(8,128)} fusion(s32[16384]{0:T(1024)S(1)} %bitcast.957, f32[16384,8]{1,0:T(8,128)} %copy.267, f32[]{:T(128)} %constant.207.clone.1), kind=kCustom, calls=%fused_computation.9 | custom fusion | flops 131072 | bytes 262656 | tf_op jit(solution)/shard_map/scatter-add | solution.py:135
  741.5 28.7 %slice_reduce_fusion = (f32[8192]{0:T(1024)}, f32[8192]{0:T(1024)S(1)}, f32[8192]{0:T(1024)S(1)}, f32[8192]{0:T(1024)S(1)}, f32[8192]{0:T(1024)S(1)}, /*index=5*...) fusion(f32[8,8192]{0,1:T(8,128)} %scatter_custom_fusion), kind=kLoop, calls=%fused_computation.1 | loop fusion | bytes 524288 | tf_op jit(solution)/shard_map/slice | solution.py:165
  789.1 5.8 collective-permute-start.5
  796.5 5.2 collective-permute-done.8
  803.3 5.5 collective-permute-start.10
  814.3 5.2 collective-permute-done.12
  821.1 5.5 collective-permute-start.14
  826.8 5.2 collective-permute-start.13
  833.7 5.2 collective-permute-done.16
  840.5 5.5 collective-permute-start.18
  857.4 4.3 collective-permute-start.22
  863.8 4.8 collective-permute-done.19
  870.1 5.7 collective-permute-start.21
  877.6 5.1 collective-permute-start.26
  884.3 5.4 collective-permute-done.23
  891.3 6.5 collective-permute-start.25
  900.9 6.4 collective-permute-start.29
  908.9 6.0 collective-permute-start.30
  929.9 188.9 %reduce-scatter.3.cloned.1.call-done = f32[2,8,128]{2,1,0:T(8,128)} async-done(((f32[2,32,128]{2,1,0:T(8,128)}), f32[2,8,128]{2,1,0:T(8,128)}) %reduce-scatter.3.cloned.1.call-update) | async-done | bytes 8208 | tf_op jit(solution)/shard_map/reduce_scatter | solution.py:169
  1118.8 28.9 %reduce-scatter.5.cloned.1.call-done = f32[2,8,128]{2,1,0:T(8,128)} async-done(((f32[2,32,128]{2,1,0:T(8,128)}), f32[2,8,128]{2,1,0:T(8,128)}) %reduce-scatter.5.cloned.1.call-update) | async-done | bytes 8208 | tf_op jit(solution)/shard_map/reduce_scatter | solution.py:170
  (233 shorter events, 79.2 us)
Async XLA Ops:
  7.2 1111.7 %reduce-scatter.3.cloned.1.call-start = ((), (), s32[]{:S(2)}) async-start(), calls=%async_computation.2 | async-start | bytes 40960 | tf_op jit(solution)/shard_map/reduce_scatter | solution.py:169
  8.0 766.6 %collective-permute-start.2 = (f32[2,2,1,32,128]{4,3,0,2,1:T(8,128)S(1)}, f32[2,2,1,32,128]{4,3,0,2,1:T(8,128)S(1)}, u32[]{:S(2)}, u32[]{:S(2)}) collective-permute-start(f32[2,2,1,32,128]{4,3,0,2,1:T(8,128)S(1)} %get-tuple-element.218), channel_id=1, source_target_pairs={{0,1},{1,2},{2,3},{3,4},{4,5},{5,6},{6,7},{7,8},{8,9},{9,10},{10,1... | collective-permute-start | bytes 196616 | tf_op jit(solution)/shard_map/ppermute | solution.py:12
  14.3 760.5 %collective-permute-start = (f32[2,1,32,128]{3,2,0,1:T(8,128)S(1)}, f32[2,1,32,128]{3,2,0,1:T(8,128)S(1)}, u32[]{:S(2)}, u32[]{:S(2)}) collective-permute-start(f32[2,1,32,128]{3,2,0,1:T(8,128)S(1)} %get-tuple-element.213), channel_id=1, source_target_pairs={{1,0},{2,1},{3,2},{4,3},{5,4},{6,5},{7,6},{8,7},{9,8},{10,9},{11,1... | collective-permute-start | bytes 98312 | tf_op jit(solution)/shard_map/ppermute | solution.py:12
  781.3 7.6 collective-permute-start.3
  785.8 9.1 collective-permute-start.6
  789.1 7.4 collective-permute-start.5
  801.9 6.9 collective-permute-start.7
  803.3 9.4 collective-permute-start.10
  819.7 6.9 collective-permute-start.11
  821.1 11.0 collective-permute-start.14
  826.8 6.8 collective-permute-start.13
  839.0 6.9 collective-permute-start.15
  840.5 9.4 collective-permute-start.18
  868.8 7.9 collective-permute-start.24
  870.1 6.6 collective-permute-start.21
  877.6 6.7 collective-permute-start.26
  882.8 6.9 collective-permute-start.23
  890.0 8.8 collective-permute-start.28
  891.3 7.5 collective-permute-start.25
  899.6 7.8 collective-permute-start.27
  900.9 14.0 %collective-permute-start.29 = (f32[2,2,1,32,128]{4,3,2,0,1:T(8,128)S(1)}, f32[2,2,1,32,128]{4,3,2,0,1:T(8,128)S(1)}, u32[]{:S(2)}, u32[]{:S(2)}) collective-permute-start(f32[2,2,1,32,128]{4,3,2,0,1:T(8,128)S(1)} %fusion.17), channel_id=1, source_target_pairs={{0,1},{1,2},{2,3},{3,4},{4,5},{5,6},{6,7},{7,8},{8,9},{9,10},{10,1... | collective-permute-start | bytes 196616 | tf_op jit(solution)/shard_map/ppermute | solution.py:12
  908.9 9.5 collective-permute-start.30
  917.1 7.2 collective-permute-start.31
  919.1 228.6 %reduce-scatter.5.cloned.1.call-start = ((), (), s32[]{:S(2)}) async-start(), calls=%async_computation.3 | async-start | bytes 40960 | tf_op jit(solution)/shard_map/reduce_scatter | solution.py:170
  (18 other events, 206.4 us)
Sparse Core Ops, SparseCore 0:
  919.3 199.5 reduce-scatter.2
  1122.4 25.2 reduce-scatter.4
where the time goes:
time: 1160 us; the launch traced here: 1150 us
  blocking collectives  600 us (52%)
  waiting for transfers between devices  255 us (22%)
  other arithmetic  141 us (12%)
  starting transfers between devices  102 us (9%)
  local copies, waits for them, and re-layouts  40.4 us (3%)
  between operations  16 us (1%)
    all_gather x1, blocking collectives, shards(): lax.all_gather(targets, 'slab', axis=1, tiled=True)  305 us
    all_gather x1, blocking collectives, shards(): lax.all_gather(traces, 'slab', axis=1, tiled=True)  295 us
    reduce_scatter x1, waiting for transfers between devices, shards(): lax.psum_scatter(grad_lambda, 'shot', scatter_dimension=1, tiled=True)  189 us
    scatter-add x1, other arithmetic, shards(): jnp.zeros((steps_total, cell_count), jnp.float32).at[:, cell_index]  115 us
    ppermute x32, starting transfers between devices, from_behind(): lax.ppermute(value, axis, [(source, source + steps) for source in range(i...  102 us
    ppermute x32, waiting for transfers between devices, from_behind(): lax.ppermute(value, axis, [(source, source + steps) for source in range(i...  37.4 us
    reduce_scatter x1, waiting for transfers between devices, shards(): lax.psum_scatter(grad_shear, 'shot', scatter_dimension=1, tiled=True)  28.9 us
    slice x1, local copies, waits for them, and re-layouts, shards(): receiver_push[step_index]  28.7 us
  transfers between devices with their start and end apart: 34, of which 12 were waited for; matrix products, arithmetic and copies ran while one was open for 15% of the time, Pallas kernels for 0%

commit v1 on v0

v1 whole, which is shorter than its diff:
```python
import functools

import jax
import jax.numpy as jnp
from jax import lax
from jax.experimental import pallas as pl
from jax.experimental.pallas import tpu as pltpu
from jax.sharding import PartitionSpec as P

TIME_STEP = 0.3
CAP = 2
LANES = 128


def reach_steps(steps, planes, reach):
    counts = {}
    for e in range(-reach, reach + 1):
        gap = planes * (abs(e) - 1) + 1 if e else 0
        counts[e] = max(0, steps - gap)
    return counts


def message_lanes(counts):
    lanes, at = {}, 0
    for e in sorted(counts, key=abs):
        for slot in range(CAP):
            lanes[e, slot] = at
            at += 1 + counts[e]
    return lanes, at


def split3(x):
    hi = x.astype(jnp.bfloat16)
    rest = x - hi.astype(jnp.float32)
    mid = rest.astype(jnp.bfloat16)
    low = (rest - mid.astype(jnp.float32)).astype(jnp.bfloat16)
    return hi, mid, low


def dot_onehot(values, onehot, dims):
    hi, mid, low = split3(values)
    hot = onehot.astype(jnp.bfloat16)
    go = lambda part: lax.dot_general(part, hot, dims, preferred_element_type=jnp.float32)
    return go(hi) + (go(mid) + go(low))


def onehot_dot(onehot, values, dims):
    hi, mid, low = split3(values)
    hot = onehot.astype(jnp.bfloat16)
    go = lambda part: lax.dot_general(hot, part, dims, preferred_element_type=jnp.float32)
    return go(hi) + (go(mid) + go(low))


def letters_kernel(counts, lanes, reach, trace_ref, slab_ref, cell_ref, out_ref, rows_ref):
    steps, count = trace_ref.shape
    slab_col = jnp.broadcast_to(slab_ref[...], (count, count))
    slab_row = slab_col.astype(jnp.float32).T.astype(jnp.int32)
    sub = lax.broadcasted_iota(jnp.int32, (count, count), 0)
    lane = lax.broadcasted_iota(jnp.int32, (count, count), 1)
    same = jnp.where((slab_col == slab_row) & (lane < sub), 1.0, 0.0)
    slot_of = jnp.sum(same, axis=1, keepdims=True)
    table = jnp.concatenate(
        [trace_ref[...], cell_ref[...].astype(jnp.float32), jnp.zeros((16 - steps - 1, count), jnp.float32)], axis=0
    )
    src = lax.broadcasted_iota(jnp.int32, (16, LANES), 0)
    dst = lax.broadcasted_iota(jnp.int32, (16, LANES), 1)
    spread = jnp.zeros((16, LANES), jnp.float32)
    slot_lane = jnp.zeros((1, LANES), jnp.float32)
    one_lane = lax.broadcasted_iota(jnp.int32, (1, LANES), 1)
    for (e, slot), at in lanes.items():
        n = counts[e]
        spread = jnp.where((dst == at) & (src == steps), 1.0, spread)
        spread = jnp.where((dst > at) & (dst <= at + n) & (src == dst - at - 1), 1.0, spread)
        slot_lane = jnp.where((one_lane >= at) & (one_lane <= at + n), float(slot), slot_lane)
    wide = dot_onehot(table, spread, (((0,), (0,)), ((), ())))
    wide = jnp.where(slot_of == slot_lane, wide, 0.0)
    pick = jnp.where(slab_row == sub, 1.0, 0.0)
    rows = onehot_dot(pick, wide, (((1,), (0,)), ((), ())))
    rows_ref[...] = jnp.zeros_like(rows_ref)
    rows_ref[8 : 8 + count] = rows
    letter = jnp.zeros((count, LANES), jnp.float32)
    for e in range(-reach, reach + 1):
        start, end = lanes[e, 0], lanes[e, CAP - 1] + counts[e]
        letter = jnp.where((lane >= start) & (lane <= end), rows_ref[8 + e : 8 + e + count], letter)
    out_ref[...] = letter


def window_kernel(
    counts, lanes, reach, steps, meta_ref, wavelet_ref, *refs
):
    blocks = refs[: 2 * reach]
    own_f, own_a, lam_in, mu_in, buo_in, letters_ref, end_ref, grad_ref, state, par, push = refs[2 * reach :]
    planes, rows, depth = lam_in.shape
    halo = planes * reach
    for i, block in enumerate(blocks):
        e = i - reach if i < reach else i - reach + 1
        at = halo + planes * e
        for f in range(2):
            for c in range(9):
                state[f, c, at : at + planes] = block[9 * f + c]
        for c in range(3):
            par[c, at : at + planes] = block[18 + c]
    for c in range(9):
        state[0, c, halo : halo + planes] = own_f[c]
        state[1, c, halo : halo + planes] = own_a[c]
    for c, ref in enumerate((lam_in, mu_in, buo_in)):
        par[c, halo : halo + planes] = ref[...]
    letters = letters_ref[...]
    letters_t = letters.T
    sources = letters.shape[0]
    lane_iota = lax.broadcasted_iota(jnp.int32, (sources, depth), 1)
    row_iota = lax.broadcasted_iota(jnp.int32, (planes * rows, sources), 0)
    for e in range(-reach, reach + 1):
        n = counts[e]
        lefts, rights = [], []
        for slot in range(CAP):
            at = lanes[e, slot]
            cell_col = letters[:, at : at + 1].astype(jnp.int32)
            rights.append(jnp.where(lane_iota == (cell_col & (depth - 1)), 1.0, 0.0))
            cell_row = letters_t[at : at + 1, :].astype(jnp.int32) // depth
            hit = row_iota == cell_row
            lefts.append(
                jnp.concatenate([jnp.where(hit, letters_t[at + 1 + k : at + 2 + k, :], 0.0) for k in range(n)], axis=0)
            )
        left = jnp.concatenate(lefts, axis=1)
        right = jnp.concatenate(rights, axis=0)
        sums = TIME_STEP * dot_onehot(left, right, (((1,), (0,)), ((), ())))
        for k in range(n):
            push[k, halo + planes * e : halo + planes * (e + 1)] = sums[
                k * planes * rows : (k + 1) * planes * rows
            ].reshape(planes, rows, depth)

    y_iota = lax.broadcasted_iota(jnp.int32, (rows, depth), 0)
    z_iota = lax.broadcasted_iota(jnp.int32, (rows, depth), 1)
    y_first, y_last = y_iota == 0, y_iota == rows - 1
    z_first, z_last = z_iota == 0, z_iota == depth - 1

    def prev_y(x):
        return jnp.where(y_first, 0.0, pltpu.roll(x, 1, 0))

    def next_y(x):
        return jnp.where(y_last, 0.0, pltpu.roll(x, rows - 1, 0))

    def prev_z(x):
        return jnp.where(z_first, 0.0, pltpu.roll(x, 1, 1))

    def next_z(x):
        return jnp.where(z_last, 0.0, pltpu.roll(x, depth - 1, 1))

    def velocity(p, along_x, across):
        factor = TIME_STEP * par[2, p]
        for f in range(2):
            sxy, sxz = state[f, 6, p], state[f, 7, p]
            if along_x:
                accel = (state[f, 3, p + 1] - state[f, 3, p]) + (sxy - prev_y(sxy)) + (sxz - prev_z(sxz))
                state[f, 0, p] = state[f, 0, p] - factor * accel
            if across:
                syy, szz, syz = state[f, 4, p], state[f, 5, p], state[f, 8, p]
                accel = (sxy - state[f, 6, p - 1]) + (next_y(syy) - syy) + (syz - prev_z(syz))
                state[f, 1, p] = state[f, 1, p] - factor * accel
                accel = (sxz - state[f, 7, p - 1]) + (syz - prev_y(syz)) + (next_z(szz) - szz)
                state[f, 2, p] = state[f, 2, p] - factor * accel

    def stress(p, k, image):
        lam = TIME_STEP * par[0, p]
        mu = TIME_STEP * par[1, p]
        twice = 2.0 * mu
        strains = []
        for f in range(2):
            vx, vy, vz = state[f, 0, p], state[f, 1, p], state[f, 2, p]
            exx = vx - state[f, 0, p - 1]
            eyy = vy - prev_y(vy)
            ezz = vz - prev_z(vz)
            exy = (next_y(vx) - vx) + (state[f, 1, p + 1] - vy)
            exz = (next_z(vx) - vx) + (state[f, 2, p + 1] - vz)
            eyz = (next_z(vy) - vy) + (next_y(vz) - vz)
            tr = exx + eyy + ezz
            volume = lam * tr
            if f == 1:
                volume = volume + push[k, p]
            state[f, 3, p] = state[f, 3, p] - (volume + twice * exx)
            state[f, 4, p] = state[f, 4, p] - (volume + twice * eyy)
            state[f, 5, p] = state[f, 5, p] - (volume + twice * ezz)
            state[f, 6, p] = state[f, 6, p] - mu * exy
            state[f, 7, p] = state[f, 7, p] - mu * exz
            state[f, 8, p] = state[f, 8, p] - mu * eyz
            strains.append((exx, eyy, ezz, exy, exz, eyz, tr))
        if image:
            (axx, ayy, azz, axy, axz, ayz, atr), (bxx, byy, bzz, bxy, bxz, byz, btr) = strains
            return atr * btr, 2.0 * (axx * bxx + ayy * byy + azz * bzz) + axy * bxy + axz * bxz + ayz * byz
        return None

    cell = meta_ref[0]
    src_plane = cell // (rows * depth) - planes * meta_ref[1] + halo
    src_at = cell % (rows * depth)
    spot = jnp.where(y_iota * depth + z_iota == src_at, TIME_STEP, 0.0)

    totals = [[jnp.zeros((rows, depth), jnp.float32)] * 2 for _ in range(planes)]
    for k in range(steps):
        m = steps - 1 - k
        low, high = halo - m, halo + planes + m
        velocity(low - 1, True, False)

        @pl.loop(low, high)
        def _(p):
            velocity(p, True, True)

        velocity(high, False, True)
        if m:
            @pl.loop(low, halo)
            def _(p):
                stress(p, k, False)

            @pl.loop(halo + planes, high)
            def _(p):
                stress(p, k, False)

        for p in range(planes):
            first, second = stress(halo + p, k, True)
            totals[p] = [totals[p][0] + first, totals[p][1] + second]

        @pl.when((src_plane >= low) & (src_plane < high))
        def _():
            shot = wavelet_ref[k] * spot
            for c in (3, 4, 5):
                state[0, c, src_plane] = state[0, c, src_plane] - shot

    for c in range(9):
        end_ref[c] = state[1, c, halo : halo + planes]
    share = rows // grad_ref.shape[0]
    for p in range(planes):
        for g in range(2):
            total = TIME_STEP * totals[p][g]
            for j in range(grad_ref.shape[0]):
                grad_ref[j, g, p] = total[j * share : (j + 1) * share]


def vmem():
    return pl.BlockSpec(memory_space=pltpu.VMEM)


def smem():
    return pl.BlockSpec(memory_space=pltpu.SMEM)


def shards(
    lame_lambda,
    lame_mu,
    buoyancy,
    forward_state,
    adjoint_state,
    source_wavelet,
    source_cell,
    residual_traces,
    receiver_slab,
    receiver_cell,
):
    planes, rows, depth = lame_lambda.shape
    steps = source_wavelet.shape[1]
    slabs = lax.axis_size("slab")
    shots = lax.axis_size("shot")
    reach = -(-steps // planes)
    counts = reach_steps(steps, planes, reach)
    lanes, _ = message_lanes(counts)
    my_slab = lax.axis_index("slab")

    letters = pl.pallas_call(
        functools.partial(letters_kernel, counts, lanes, reach),
        out_shape=jax.ShapeDtypeStruct((slabs, LANES), jnp.float32),
        in_specs=[vmem()] * 3,
        out_specs=vmem(),
        scratch_shapes=[pltpu.VMEM((slabs + 16, LANES), jnp.float32)],
        name="letters",
    )(residual_traces[0], receiver_slab, receiver_cell[None, :])

    block = jnp.concatenate(
        [forward_state[0], adjoint_state[0], lame_lambda[None], lame_mu[None], buoyancy[None]], axis=0
    )
    offsets = [e for e in range(-reach, reach + 1) if e]
    near = {}
    for e in offsets:
        near[e] = lax.ppermute(
            block, "slab", [(i + e, i) for i in range(slabs) if 0 <= i + e < slabs]
        )
    got = lax.all_to_all(letters, "slab", 0, 0, tiled=True)

    extent = planes + 2 * planes * reach
    meta = jnp.concatenate([source_cell, my_slab[None].astype(jnp.int32)])
    end, grads = pl.pallas_call(
        functools.partial(window_kernel, counts, lanes, reach, steps),
        out_shape=(
            jax.ShapeDtypeStruct((9, planes, rows, depth), jnp.float32),
            jax.ShapeDtypeStruct((shots, 2, planes, rows // shots, depth), jnp.float32),
        ),
        in_specs=[smem(), smem()] + [vmem()] * (2 * reach + 6),
        out_specs=(vmem(), vmem()),
        scratch_shapes=[
            pltpu.VMEM((2, 9, extent, rows, depth), jnp.float32),
            pltpu.VMEM((3, extent, rows, depth), jnp.float32),
            pltpu.VMEM((steps, extent, rows, depth), jnp.float32),
        ],
        compiler_params=pltpu.CompilerParams(vmem_limit_bytes=48 * 1024 * 1024),
        name="window",
    )(
        meta,
        source_wavelet[0],
        *[near[e] for e in offsets],
        forward_state[0],
        adjoint_state[0],
        lame_lambda,
        lame_mu,
        buoyancy,
        got,
    )
    parts = lax.all_to_all(grads, "shot", 0, 0, tiled=True)
    total = jnp.sum(parts, axis=0)
    return (end[None], total[0], total[1])


def solution(mesh):
    in_specs = (
        P("slab", None, None),
        P("slab", None, None),
        P("slab", None, None),
        P("shot", None, "slab", None, None),
        P("shot", None, "slab", None, None),
        P("shot", None),
        P("shot"),
        P("shot", None, "slab"),
        P("slab", None),
        P("slab"),
    )
    out_specs = (
        P("shot", None, "slab", None, None),
        P("slab", "shot", None),
        P("slab", "shot", None),
    )
    return jax.shard_map(shards, mesh=mesh, in_specs=in_specs, out_specs=out_specs, check_vma=False)
```

time: 1160 us -> 157 us (0.14)
  blocking collectives: 600 us -> 10.2 us
  waiting for transfers between devices: 255 us -> 68.3 us
  other arithmetic: 141 us -> 0.08 us
  starting transfers between devices: 102 us -> 48.7 us
  local copies, waits for them, and re-layouts: 40.4 us -> 6.34 us
  Pallas kernels: 0 us -> 20.9 us
  between operations: 16 us -> 1.44 us
    all_gather x2 -> x0, blocking collectives: 600 us -> none  [the longest x1 305 us: shards(): lax.all_gather(targets, 'slab', axis=1, tiled=True)]
    reduce_scatter x2 -> x0, waiting for transfers between devices: 218 us -> none  [the longest x1 189 us: shards(): lax.psum_scatter(grad_lambda, 'shot', scatter_dimension=1, tiled=True)]
    scatter-add x2 -> x0, other arithmetic: 115 us -> none  [the longest x1 115 us: shards(): jnp.zeros((steps_total, cell_count), jnp.float32).at[:, cell_index]]
    ppermute x32 -> x8, starting transfers between devices: 102 us -> 22 us  [shards(): lax.ppermute(block, 'slab', [(i + e, i) for i in range(slabs) if 0 <= i +...]
    slice x60 -> x0, local copies, waits for them, and re-layouts: 35 us -> none  [the longest x1 28.7 us: shards(): receiver_push[step_index]]
    all_to_all x0 -> x1, starting transfers between devices: none -> 26.7 us  [shards(): got = lax.all_to_all(letters, 'slab', 0, 0, tiled=True)]
    all_to_all x0 -> x1, waiting for transfers between devices: none -> 26.3 us  [shards(): got = lax.all_to_all(letters, 'slab', 0, 0, tiled=True)]
    pallas_call x0 -> x2, Pallas kernels: none -> 20.9 us  [the longest x1 19 us: shards(): pl.pallas_call(functools.partial(window_kernel, counts, lanes, reach, ste...]
  transfers between devices with their start and end apart: 34 -> 9, of which waited for: 12 -> 3; matrix products, arithmetic and copies ran while one was open for 15% -> 1% of each run, Pallas kernels for 0% -> 1%
where the time goes in v1:
time: 157 us; the launch traced here: 156 us
  waiting for transfers between devices  68.3 us (44%)
  starting transfers between devices  48.7 us (31%)
  Pallas kernels  20.9 us (13%)
  blocking collectives  10.2 us (6%)
  local copies, waits for them, and re-layouts  6.34 us (4%)
    ppermute x8, waiting for transfers between devices, shards(): lax.ppermute(block, 'slab', [(i + e, i) for i in range(slabs) if 0 <= i +...  42 us
    all_to_all x1, starting transfers between devices, shards(): got = lax.all_to_all(letters, 'slab', 0, 0, tiled=True)  26.7 us
    all_to_all x1, waiting for transfers between devices, shards(): got = lax.all_to_all(letters, 'slab', 0, 0, tiled=True)  26.3 us
    ppermute x8, starting transfers between devices, shards(): lax.ppermute(block, 'slab', [(i + e, i) for i in range(slabs) if 0 <= i +...  22 us
    pallas_call x1, Pallas kernels, shards(): pl.pallas_call(functools.partial(window_kernel, counts, lanes, reach, ste...  19 us
    all_to_all x1, blocking collectives, shards(): parts = lax.all_to_all(grads, 'shot', 0, 0, tiled=True)  10.2 us
    unnamed x19, local copies, waits for them, and re-layouts  5.11 us
  transfers between devices with their start and end apart: 9, of which 3 were waited for; matrix products, arithmetic and copies ran while one was open for 1% of the time, Pallas kernels for 1%

profile of v1, /device:TPU:1, one launch (start us, length us, event | category | flops | bytes accessed | tf_op | source)
XLA Modules:
  0.0 156.0 jit_solution(7074286364352335545)
XLA Ops:
  0.6 1.7 %constant_dynamic-update-slice_fusion.1 = f32[21,2,32,128]{3,2,1,0:T(8,128)} fusion(f32[1,9,2,32,128]{4,3,2,1,0:T(8,128)} %param.13), kind=kLoop, calls=%fused_computation.4 | loop fusion | bytes 589824
  2.4 0.7 constant_dynamic-update-slice_fusion
  3.2 0.6 bitcast_dynamic-update-slice_fusion.2
  3.8 0.6 bitcast_dynamic-update-slice_fusion.1
  4.4 0.6 bitcast_dynamic-update-slice_fusion
  5.0 5.7 %collective-permute-start = (f32[21,2,32,128]{3,2,1,0:T(8,128)}, f32[21,2,32,128]{3,2,1,0:T(8,128)S(1)}, u32[]{:S(2)}, u32[]{:S(2)}) collective-permute-start(f32[21,2,32,128]{3,2,1,0:T(8,128)} %bitcast_dynamic-update-slice_fusion), channel_id=1, source_target_pairs={{0,4},{1,5},{2,6},{3,7},{4,8},{5,9},{6,10},{7,11},{8,12},{9,13},{1... | collective-permute-start | bytes 2064392 | tf_op jit(solution)/shard_map/ppermute | solution.py:282
  10.7 4.8 %collective-permute-start.1 = (f32[21,2,32,128]{3,2,1,0:T(8,128)}, f32[21,2,32,128]{3,2,1,0:T(8,128)S(1)}, u32[]{:S(2)}, u32[]{:S(2)}) collective-permute-start(f32[21,2,32,128]{3,2,1,0:T(8,128)} %bitcast_dynamic-update-slice_fusion), channel_id=1, source_target_pairs={{0,3},{1,4},{2,5},{3,6},{4,7},{5,8},{6,9},{7,10},{8,11},{9,12},{10... | collective-permute-start | bytes 2064392 | tf_op jit(solution)/shard_map/ppermute | solution.py:282
  15.5 2.6 %collective-permute-start.2 = (f32[21,2,32,128]{3,2,1,0:T(8,128)}, f32[21,2,32,128]{3,2,1,0:T(8,128)S(1)}, u32[]{:S(2)}, u32[]{:S(2)}) collective-permute-start(f32[21,2,32,128]{3,2,1,0:T(8,128)} %bitcast_dynamic-update-slice_fusion), channel_id=1, source_target_pairs={{0,2},{1,3},{2,4},{3,5},{4,6},{5,7},{6,8},{7,9},{8,10},{9,11},{10,... | collective-permute-start | bytes 2064392 | tf_op jit(solution)/shard_map/ppermute | solution.py:282
  18.1 3.8 %collective-permute-start.3 = (f32[21,2,32,128]{3,2,1,0:T(8,128)}, f32[21,2,32,128]{3,2,1,0:T(8,128)S(1)}, u32[]{:S(2)}, u32[]{:S(2)}) collective-permute-start(f32[21,2,32,128]{3,2,1,0:T(8,128)} %bitcast_dynamic-update-slice_fusion), channel_id=1, source_target_pairs={{0,1},{1,2},{2,3},{3,4},{4,5},{5,6},{6,7},{7,8},{8,9},{9,10},{10,1... | collective-permute-start | bytes 2064392 | tf_op jit(solution)/shard_map/ppermute | solution.py:282
  21.9 1.3 collective-permute-start.4
  23.2 29.8 %collective-permute-done.refs_0_ = f32[21,2,32,128]{3,2,1,0:T(8,128)S(1)} collective-permute-done((f32[21,2,32,128]{3,2,1,0:T(8,128)}, f32[21,2,32,128]{3,2,1,0:T(8,128)S(1)}, u32[]{:S(2)}, u32[]{:S(2)}) %collective-permute-start) | collective-permute-done | bytes 688160 | tf_op jit(solution)/shard_map/ppermute | solution.py:282
  53.0 1.3 collective-permute-start.5
  54.3 1.3 collective-permute-start.6
  55.6 12.1 %collective-permute-done.2.refs_2_ = f32[21,2,32,128]{3,2,1,0:T(8,128)S(1)} collective-permute-done((f32[21,2,32,128]{3,2,1,0:T(8,128)}, f32[21,2,32,128]{3,2,1,0:T(8,128)S(1)}, u32[]{:S(2)}, u32[]{:S(2)}) %collective-permute-start.2) | collective-permute-done | bytes 688160 | tf_op jit(solution)/shard_map/ppermute | solution.py:282
  67.7 1.3 collective-permute-start.7
  69.0 0.7 copy.14.slab_ref
  69.8 2.0 %letters.1 = f32[128,128]{1,0:T(8,128)} custom-call(f32[8,128]{1,0:T(8,128)} %bitcast.28, s32[128,1]{1,0:T(8,128)} %copy.14.slab_ref, s32[1,128]{1,0:T(1,128)} %bitcast.29), custom_call_target="tpu_custom_call" | custom-call | tf_op jit(solution)/shard_map/letters/pallas_call | solution.py:267
  71.7 26.7 %all-to-all-start = ((f32[128,1,128]{2,1,0:T(1,128)}), f32[128,1,128]{2,1,0:T(1,128)S(1)}, u32[]{:S(2)}, u32[]{:S(2)}) async-start(f32[128,1,128]{2,1,0:T(1,128)} %bitcast.27), calls=%async_computation | async-start | bytes 131072 | tf_op jit(solution)/shard_map/all_to_all | solution.py:285
  99.1 0.1 pad_add_fusion.meta_ref
  99.2 26.3 %all-to-all-done = f32[128,1,128]{2,1,0:T(1,128)S(1)} async-done(((f32[128,1,128]{2,1,0:T(1,128)}), f32[128,1,128]{2,1,0:T(1,128)S(1)}, u32[]{:S(2)}, u32[]{:S(2)}) %all-to-all-start) | async-done | bytes 65568 | tf_op jit(solution)/shard_map/all_to_all | solution.py:285
  125.5 0.6 copy-done.5
  126.2 19.0 %window.1 = (f32[9,2,32,128]{3,2,1,0:T(8,128)}, f32[4,2,2,8,128]{4,3,2,1,0:T(8,128)S(1)}) custom-call(s32[2]{0:T(128)S(1)} %pad_add_fusion.meta_ref, f32[8]{0:T(128)S(1)} %bitcast.26, f32[21,2,32,128]{3,2,1,0:T(8,128)S(1)} %collective-permute-done.refs_0_, f32[21,2,32,128]{3,2,1,0:T(8,128)S(1)} %collective-permute-done.1.refs_1_, ...), custom_call_target="tpu_custom_call" | custom-call | tf_op jit(solution)/shard_map/window/pallas_call | solution.py:289
  145.1 10.2 %all_to_all.16 = f32[4,2,2,8,128]{4,3,2,1,0:T(8,128)S(1)} all-to-all(f32[4,2,2,8,128]{4,3,2,1,0:T(8,128)S(1)} %get-tuple-element.6), channel_id=1, replica_groups=mesh['shot'=4,'slab'=128] {'shot'}, dimensions={0} | all-to-all | bytes 131072 | tf_op jit(solution)/shard_map/all_to_all | solution.py:315
  155.4 0.6 slice_bitcast_fusion
  (20 shorter events, 0.1 us)
Async XLA Ops:
  0.6 1.8 %copy-start.1 = (f32[1,9,2,32,128]{4,3,2,1,0:T(8,128)S(1)}, f32[1,9,2,32,128]{4,3,2,1,0:T(8,128)}, u32[]{:S(2)}) copy-start(f32[1,9,2,32,128]{4,3,2,1,0:T(8,128)} %param.14) | copy-start | bytes 884740
  2.4 0.8 copy-start.2
  2.4 1.4 copy-start.3
  2.4 2.0 %copy-start.4 = (f32[2,32,128]{2,1,0:T(8,128)S(1)}, f32[2,32,128]{2,1,0:T(8,128)}, u32[]{:S(2)}) copy-start(f32[2,32,128]{2,1,0:T(8,128)} %refs_12_.1) | copy-start | bytes 98308
  2.4 66.6 %copy-start.6 = (s32[128,1]{0,1:T(1,128)S(1)}, s32[128,1]{0,1:T(1,128)}, u32[]{:S(2)}) copy-start(s32[128,1]{0,1:T(1,128)} %param.18) | copy-start | bytes 1540
  3.2 122.4 %copy-start = (f32[1,9,2,32,128]{4,3,2,1,0:T(8,128)S(1)}, f32[1,9,2,32,128]{4,3,2,1,0:T(8,128)}, u32[]{:S(2)}) copy-start(f32[1,9,2,32,128]{4,3,2,1,0:T(8,128)} %param.13) | copy-start | bytes 884740
  5.0 48.0 %collective-permute-start = (f32[21,2,32,128]{3,2,1,0:T(8,128)}, f32[21,2,32,128]{3,2,1,0:T(8,128)S(1)}, u32[]{:S(2)}, u32[]{:S(2)}) collective-permute-start(f32[21,2,32,128]{3,2,1,0:T(8,128)} %bitcast_dynamic-update-slice_fusion), channel_id=1, source_target_pairs={{0,4},{1,5},{2,6},{3,7},{4,8},{5,9},{6,10},{7,11},{8,12},{9,13},{1... | collective-permute-start | bytes 2064392 | tf_op jit(solution)/shard_map/ppermute | solution.py:282
  10.7 43.6 %collective-permute-start.1 = (f32[21,2,32,128]{3,2,1,0:T(8,128)}, f32[21,2,32,128]{3,2,1,0:T(8,128)S(1)}, u32[]{:S(2)}, u32[]{:S(2)}) collective-permute-start(f32[21,2,32,128]{3,2,1,0:T(8,128)} %bitcast_dynamic-update-slice_fusion), channel_id=1, source_target_pairs={{0,3},{1,4},{2,5},{3,6},{4,7},{5,8},{6,9},{7,10},{8,11},{9,12},{10... | collective-permute-start | bytes 2064392 | tf_op jit(solution)/shard_map/ppermute | solution.py:282
  15.5 52.2 %collective-permute-start.2 = (f32[21,2,32,128]{3,2,1,0:T(8,128)}, f32[21,2,32,128]{3,2,1,0:T(8,128)S(1)}, u32[]{:S(2)}, u32[]{:S(2)}) collective-permute-start(f32[21,2,32,128]{3,2,1,0:T(8,128)} %bitcast_dynamic-update-slice_fusion), channel_id=1, source_target_pairs={{0,2},{1,3},{2,4},{3,5},{4,6},{5,7},{6,8},{7,9},{8,10},{9,11},{10,... | collective-permute-start | bytes 2064392 | tf_op jit(solution)/shard_map/ppermute | solution.py:282
  18.1 107.4 %collective-permute-start.3 = (f32[21,2,32,128]{3,2,1,0:T(8,128)}, f32[21,2,32,128]{3,2,1,0:T(8,128)S(1)}, u32[]{:S(2)}, u32[]{:S(2)}) collective-permute-start(f32[21,2,32,128]{3,2,1,0:T(8,128)} %bitcast_dynamic-update-slice_fusion), channel_id=1, source_target_pairs={{0,1},{1,2},{2,3},{3,4},{4,5},{5,6},{6,7},{7,8},{8,9},{9,10},{10,1... | collective-permute-start | bytes 2064392 | tf_op jit(solution)/shard_map/ppermute | solution.py:282
  21.9 103.6 %collective-permute-start.4 = (f32[21,2,32,128]{3,2,1,0:T(8,128)}, f32[21,2,32,128]{3,2,1,0:T(8,128)}, u32[]{:S(2)}, u32[]{:S(2)}) collective-permute-start(f32[21,2,32,128]{3,2,1,0:T(8,128)} %bitcast_dynamic-update-slice_fusion), channel_id=1, source_target_pairs={{1,0},{2,1},{3,2},{4,3},{5,4},{6,5},{7,6},{8,7},{9,8},{10,9},{11,1... | collective-permute-start | bytes 2064392 | tf_op jit(solution)/shard_map/ppermute | solution.py:282
  53.0 72.5 %collective-permute-start.5 = (f32[21,2,32,128]{3,2,1,0:T(8,128)}, f32[21,2,32,128]{3,2,1,0:T(8,128)}, u32[]{:S(2)}, u32[]{:S(2)}) collective-permute-start(f32[21,2,32,128]{3,2,1,0:T(8,128)} %bitcast_dynamic-update-slice_fusion), channel_id=1, source_target_pairs={{2,0},{3,1},{4,2},{5,3},{6,4},{7,5},{8,6},{9,7},{10,8},{11,9},{12,... | collective-permute-start | bytes 2064392 | tf_op jit(solution)/shard_map/ppermute | solution.py:282
  54.3 71.2 %collective-permute-start.6 = (f32[21,2,32,128]{3,2,1,0:T(8,128)}, f32[21,2,32,128]{3,2,1,0:T(8,128)}, u32[]{:S(2)}, u32[]{:S(2)}) collective-permute-start(f32[21,2,32,128]{3,2,1,0:T(8,128)} %bitcast_dynamic-update-slice_fusion), channel_id=1, source_target_pairs={{3,0},{4,1},{5,2},{6,3},{7,4},{8,5},{9,6},{10,7},{11,8},{12,9},{13... | collective-permute-start | bytes 2064392 | tf_op jit(solution)/shard_map/ppermute | solution.py:282
  67.7 57.8 %collective-permute-start.7 = (f32[21,2,32,128]{3,2,1,0:T(8,128)}, f32[21,2,32,128]{3,2,1,0:T(8,128)}, u32[]{:S(2)}, u32[]{:S(2)}) collective-permute-start(f32[21,2,32,128]{3,2,1,0:T(8,128)} %bitcast_dynamic-update-slice_fusion), channel_id=1, source_target_pairs={{4,0},{5,1},{6,2},{7,3},{8,4},{9,5},{10,6},{11,7},{12,8},{13,9},{1... | collective-permute-start | bytes 2064392 | tf_op jit(solution)/shard_map/ppermute | solution.py:282
  71.7 53.7 %all-to-all-start = ((f32[128,1,128]{2,1,0:T(1,128)}), f32[128,1,128]{2,1,0:T(1,128)S(1)}, u32[]{:S(2)}, u32[]{:S(2)}) async-start(f32[128,1,128]{2,1,0:T(1,128)} %bitcast.27), calls=%async_computation | async-start | bytes 131072 | tf_op jit(solution)/shard_map/all_to_all | solution.py:285
  125.5 0.7 copy-start.5

commit v2 on v1

v2 whole, which is shorter than its diff:
```python
import functools

import jax
import jax.numpy as jnp
from jax import lax
from jax.experimental import pallas as pl
from jax.experimental.pallas import tpu as pltpu
from jax.sharding import PartitionSpec as P

TIME_STEP = 0.3
CAP = 2
LANES = 128
FIELDS = 21
NOTES = 16


def reach_steps(steps, planes, reach):
    counts = {}
    for e in range(-reach, reach + 1):
        gap = planes * (abs(e) - 1) + 1 if e else 0
        counts[e] = max(0, steps - gap)
    return counts


def message_lanes(counts):
    lanes, at = {}, 0
    for e in sorted(counts, key=abs):
        for slot in range(CAP):
            lanes[e, slot] = at
            at += 1 + counts[e]
    return lanes, at


def split3(x):
    hi = x.astype(jnp.bfloat16)
    rest = x - hi.astype(jnp.float32)
    mid = rest.astype(jnp.bfloat16)
    low = (rest - mid.astype(jnp.float32)).astype(jnp.bfloat16)
    return hi, mid, low


def dot_onehot(values, onehot, dims):
    hi, mid, low = split3(values)
    hot = onehot.astype(jnp.bfloat16)
    go = lambda part: lax.dot_general(part, hot, dims, preferred_element_type=jnp.float32)
    return go(hi) + (go(mid) + go(low))


def onehot_dot(onehot, values, dims):
    hi, mid, low = split3(values)
    hot = onehot.astype(jnp.bfloat16)
    go = lambda part: lax.dot_general(hot, part, dims, preferred_element_type=jnp.float32)
    return go(hi) + (go(mid) + go(low))


def letters_kernel(counts, lanes, reach, steps, note_ref, out_ref, rows_ref):
    count = note_ref.shape[1]
    notes = note_ref[...]
    slab_row = jnp.broadcast_to(notes[steps : steps + 1], (count, count))
    slab_col = slab_row.T
    sub = lax.broadcasted_iota(jnp.int32, (count, count), 0)
    lane = lax.broadcasted_iota(jnp.int32, (count, count), 1)
    same = jnp.where((slab_col == slab_row) & (lane < sub), 1.0, 0.0)
    slot_of = jnp.sum(same, axis=1, keepdims=True)
    src = lax.broadcasted_iota(jnp.int32, (NOTES, LANES), 0)
    dst = lax.broadcasted_iota(jnp.int32, (NOTES, LANES), 1)
    spread = jnp.zeros((NOTES, LANES), jnp.float32)
    slot_lane = jnp.zeros((1, LANES), jnp.float32)
    one_lane = lax.broadcasted_iota(jnp.int32, (1, LANES), 1)
    for (e, slot), at in lanes.items():
        n = counts[e]
        spread = jnp.where((dst == at) & (src == steps + 1), 1.0, spread)
        spread = jnp.where((dst > at) & (dst <= at + n) & (src == dst - at - 1), 1.0, spread)
        slot_lane = jnp.where((one_lane >= at) & (one_lane <= at + n), float(slot), slot_lane)
    wide = dot_onehot(notes, spread, (((0,), (0,)), ((), ())))
    wide = jnp.where(slot_of == slot_lane, wide, 0.0)
    pick = jnp.where(slab_row == sub.astype(jnp.float32), 1.0, 0.0)
    rows = onehot_dot(pick, wide, (((1,), (0,)), ((), ())))
    rows_ref[...] = jnp.zeros_like(rows_ref)
    rows_ref[8 : 8 + count] = rows
    letter = jnp.zeros((count, LANES), jnp.float32)
    for e in range(-reach, reach + 1):
        start, end = lanes[e, 0], lanes[e, CAP - 1] + counts[e]
        letter = jnp.where((lane >= start) & (lane <= end), rows_ref[8 + e : 8 + e + count], letter)
    out_ref[...] = letter


def pack_kernel(cell_ref, f_ref, a_ref, lam_ref, mu_ref, buo_ref, trace_ref, slab_ref, spot_ref, wave_ref, out_ref):
    planes, rows, depth = lam_ref.shape
    one = planes * rows
    for f, ref in enumerate((f_ref, a_ref)):
        for c in range(9):
            at = (9 * f + c) * one
            out_ref[at : at + one] = ref[c].reshape(one, depth)
    for c, ref in enumerate((lam_ref, mu_ref, buo_ref)):
        at = (18 + c) * one
        out_ref[at : at + one] = ref[...].reshape(one, depth)
    at, steps = FIELDS * one, trace_ref.shape[0]
    out_ref[at + 8 : at + NOTES] = jnp.zeros((NOTES - 8, depth), jnp.float32)
    out_ref[at : at + steps] = trace_ref[...]
    out_ref[at + steps : at + steps + 1] = slab_ref[...].astype(jnp.float32)
    out_ref[at + steps + 1 : at + steps + 2] = spot_ref[...].astype(jnp.float32)
    out_ref[at + steps + 2 : at + steps + 3, 0:steps] = wave_ref[...]
    out_ref[at + steps + 3 : at + steps + 4] = jnp.full((1, depth), cell_ref[0], jnp.int32).astype(jnp.float32)


def window_kernel(
    counts, lanes, reach, steps, planes, rows, meta_ref, *refs
):
    mine = refs[: reach + 1]
    theirs = refs[reach + 1 : 2 * reach + 1]
    letters_ref, end_ref, grad_ref, state, push, sems = refs[2 * reach + 1 :]
    depth = state.shape[2]
    one = planes * rows
    core, slab = meta_ref[0], meta_ref[1]
    copies = []
    for o in range(reach + 1):
        at = reach + core + (2 * core - 1) * o
        copies.append(pltpu.make_async_copy(mine[o], state.at[at], sems.at[o]))
    for o in range(reach):
        at = reach + 1 - core + (1 - 2 * core) * o
        copies.append(pltpu.make_async_copy(theirs[o], state.at[at], sems.at[reach + 1 + o]))
    for copy in copies:
        copy.start()
    halo = planes * (reach + core)
    letters = letters_ref[...]
    letters_t = letters.T
    sources = letters.shape[0]
    lane_iota = lax.broadcasted_iota(jnp.int32, (sources, depth), 1)
    row_iota = lax.broadcasted_iota(jnp.int32, (one, sources), 0)
    for e in range(-reach, reach + 1):
        n = counts[e]
        lefts, rights = [], []
        for slot in range(CAP):
            at = lanes[e, slot]
            cell_col = letters[:, at : at + 1].astype(jnp.int32)
            rights.append(jnp.where(lane_iota == (cell_col & (depth - 1)), 1.0, 0.0))
            cell_row = letters_t[at : at + 1, :].astype(jnp.int32) // depth
            hit = row_iota == cell_row
            lefts.append(
                jnp.concatenate([jnp.where(hit, letters_t[at + 1 + k : at + 2 + k, :], 0.0) for k in range(n)], axis=0)
            )
        left = jnp.concatenate(lefts, axis=1)
        right = jnp.concatenate(rights, axis=0)
        sums = TIME_STEP * dot_onehot(left, right, (((1,), (0,)), ((), ())))
        for k in range(n):
            push[k, pl.ds(halo + planes * e, planes)] = sums[k * one : (k + 1) * one].reshape(planes, rows, depth)
    for copy in copies:
        copy.wait()

    y_iota = lax.broadcasted_iota(jnp.int32, (rows, depth), 0)
    z_iota = lax.broadcasted_iota(jnp.int32, (rows, depth), 1)
    y_first, y_last = y_iota == 0, y_iota == rows - 1
    z_first, z_last = z_iota == 0, z_iota == depth - 1

    def prev_y(x):
        return jnp.where(y_first, 0.0, pltpu.roll(x, 1, 0))

    def next_y(x):
        return jnp.where(y_last, 0.0, pltpu.roll(x, rows - 1, 0))

    def prev_z(x):
        return jnp.where(z_first, 0.0, pltpu.roll(x, 1, 1))

    def next_z(x):
        return jnp.where(z_last, 0.0, pltpu.roll(x, depth - 1, 1))

    class Plane:
        def __init__(self, p):
            self.block = p // planes
            self.row = (p % planes) * rows

        def where(self, f, c):
            return self.block, pl.ds(pl.multiple_of(self.row + (9 * f + c) * one, rows), rows)

        def get(self, f, c):
            return state[self.where(f, c)]

        def put(self, f, c, value):
            state[self.where(f, c)] = value

    def velocity(p, along_x, across):
        here, after, before = Plane(p), Plane(p + 1), Plane(p - 1)
        factor = TIME_STEP * here.get(2, 2)
        for f in range(2):
            sxy, sxz = here.get(f, 6), here.get(f, 7)
            if along_x:
                accel = (after.get(f, 3) - here.get(f, 3)) + (sxy - prev_y(sxy)) + (sxz - prev_z(sxz))
                here.put(f, 0, here.get(f, 0) - factor * accel)
            if across:
                syy, szz, syz = here.get(f, 4), here.get(f, 5), here.get(f, 8)
                accel = (sxy - before.get(f, 6)) + (next_y(syy) - syy) + (syz - prev_z(syz))
                here.put(f, 1, here.get(f, 1) - factor * accel)
                accel = (sxz - before.get(f, 7)) + (syz - prev_y(syz)) + (next_z(szz) - szz)
                here.put(f, 2, here.get(f, 2) - factor * accel)

    def stress(p, k, image):
        here, after, before = Plane(p), Plane(p + 1), Plane(p - 1)
        lam = TIME_STEP * here.get(2, 0)
        mu = TIME_STEP * here.get(2, 1)
        twice = 2.0 * mu
        strains = []
        for f in range(2):
            vx, vy, vz = here.get(f, 0), here.get(f, 1), here.get(f, 2)
            exx = vx - before.get(f, 0)
            eyy = vy - prev_y(vy)
            ezz = vz - prev_z(vz)
            exy = (next_y(vx) - vx) + (after.get(f, 1) - vy)
            exz = (next_z(vx) - vx) + (after.get(f, 2) - vz)
            eyz = (next_z(vy) - vy) + (next_y(vz) - vz)
            tr = exx + eyy + ezz
            volume = lam * tr
            if f == 1:
                volume = volume + push[k, p]
            here.put(f, 3, here.get(f, 3) - (volume + twice * exx))
            here.put(f, 4, here.get(f, 4) - (volume + twice * eyy))
            here.put(f, 5, here.get(f, 5) - (volume + twice * ezz))
            here.put(f, 6, here.get(f, 6) - mu * exy)
            here.put(f, 7, here.get(f, 7) - mu * exz)
            here.put(f, 8, here.get(f, 8) - mu * eyz)
            strains.append((exx, eyy, ezz, exy, exz, eyz, tr))
        if image:
            (axx, ayy, azz, axy, axz, ayz, atr), (bxx, byy, bzz, bxy, bxz, byz, btr) = strains
            return atr * btr, 2.0 * (axx * bxx + ayy * byy + azz * bzz) + axy * bxy + axz * bxz + ayz * byz
        return None

    notes = state[reach + core, FIELDS * one + steps : FIELDS * one + steps + 8]
    wave, cell = notes[2:3], jnp.max(notes[3:4]).astype(jnp.int32)
    src_plane = cell // (rows * depth) - planes * slab + halo
    src_at = cell % (rows * depth)
    spot = jnp.where(y_iota * depth + z_iota == src_at, TIME_STEP, 0.0)

    totals = [[jnp.zeros((rows, depth), jnp.float32)] * 2 for _ in range(planes)]
    for k in range(steps):
        m = steps - 1 - k
        low, high = halo - m, halo + planes + m
        velocity(low - 1, True, False)

        @pl.loop(low, high)
        def _(p):
            velocity(p, True, True)

        velocity(high, False, True)
        if m:
            @pl.loop(low, halo)
            def _(p):
                stress(p, k, False)

            @pl.loop(halo + planes, high)
            def _(p):
                stress(p, k, False)

        for p in range(planes):
            first, second = stress(halo + p, k, True)
            totals[p] = [totals[p][0] + first, totals[p][1] + second]

        @pl.when((src_plane >= low) & (src_plane < high))
        def _():
            shot = wave[:, k : k + 1] * spot
            there = Plane(src_plane)
            for c in (3, 4, 5):
                there.put(0, c, there.get(0, c) - shot)

    for c in range(9):
        at = (9 + c) * one
        end_ref[c] = state[reach + core, at : at + one].reshape(planes, rows, depth)
    shots = grad_ref.shape[0] // 2
    share = rows // shots
    for p in range(planes):
        for g in range(2):
            total = TIME_STEP * totals[p][g]
            for j in range(shots):
                for h in range(2):
                    grad_ref[2 * j + h, g, p] = jnp.where(core == h, total[j * share : (j + 1) * share], 0.0)


def vmem():
    return pl.BlockSpec(memory_space=pltpu.VMEM)


def smem():
    return pl.BlockSpec(memory_space=pltpu.SMEM)


def anywhere():
    return pl.BlockSpec(memory_space=pl.ANY)


def shards(
    lame_lambda,
    lame_mu,
    buoyancy,
    forward_state,
    adjoint_state,
    source_wavelet,
    source_cell,
    residual_traces,
    receiver_slab,
    receiver_cell,
):
    planes, rows, depth = lame_lambda.shape
    steps = source_wavelet.shape[1]
    slabs = lax.axis_size("slab")
    shots = lax.axis_size("shot")
    axes = ("shot", "slab")
    reach = -(-steps // planes)
    counts = reach_steps(steps, planes, reach)
    lanes, _ = message_lanes(counts)
    height = FIELDS * planes * rows + NOTES

    def at(s, d):
        return ((s & ~1) | (d & 1)) * slabs + ((d & ~1) | (s & 1))

    every = [(s, d) for s in range(shots) for d in range(slabs)]
    swap = [(s * slabs + d, at(s, d)) for s, d in every]
    across = [(at(s, d), at(s, d ^ 1)) for s, d in every]
    team = [[at(s, d) for d in range(slabs)] for s in range(shots)]
    pair = [[s * slabs + 2 * q + h for s in range(shots) for h in range(2)] for q in range(slabs // 2)]

    block = pl.pallas_call(
        pack_kernel,
        out_shape=jax.ShapeDtypeStruct((height, depth), jnp.float32),
        in_specs=[smem()] + [vmem()] * 9,
        out_specs=vmem(),
        name="pack",
    )(
        source_cell,
        forward_state[0],
        adjoint_state[0],
        lame_lambda,
        lame_mu,
        buoyancy,
        residual_traces[0],
        receiver_slab.reshape(1, -1),
        receiver_cell.reshape(1, -1),
        source_wavelet,
    )
    mine = [lax.ppermute(block, axes, swap)]
    for o in range(1, reach + 1):
        pairs = []
        for s, d in every:
            i = d + o if d % 2 else d - o
            if 0 <= i < slabs:
                pairs.append((s * slabs + i, at(s, d)))
        mine.append(lax.ppermute(block, axes, pairs))

    letters = pl.pallas_call(
        functools.partial(letters_kernel, counts, lanes, reach, steps),
        grid=(1,),
        out_shape=jax.ShapeDtypeStruct((slabs, LANES), jnp.float32),
        in_specs=[pl.BlockSpec((NOTES, depth), lambda i: (FIELDS * planes * rows // NOTES, 0))],
        out_specs=pl.BlockSpec((slabs, LANES), lambda i: (0, 0)),
        scratch_shapes=[pltpu.VMEM((slabs + 16, LANES), jnp.float32)],
        name="letters",
    )(mine[0])
    got = lax.all_to_all(letters, axes, 0, 0, axis_index_groups=team, tiled=True)
    *mine, got = lax.optimization_barrier((*mine, got))
    theirs = [lax.ppermute(mine[o], axes, across) for o in range(reach)]

    my_shot, my_slab = lax.axis_index("shot"), lax.axis_index("slab")
    core = my_shot & 1
    meta = jnp.stack([core, (my_slab & ~1) | core]).astype(jnp.int32)
    extent = planes * (2 * reach + 2)
    end, grads = pl.pallas_call(
        functools.partial(window_kernel, counts, lanes, reach, steps, planes, rows),
        out_shape=(
            jax.ShapeDtypeStruct((9, planes, rows, depth), jnp.float32),
            jax.ShapeDtypeStruct((2 * shots, 2, planes, rows // shots, depth), jnp.float32),
        ),
        in_specs=[smem()] + [anywhere()] * (2 * reach + 1) + [vmem()],
        out_specs=(vmem(), vmem()),
        scratch_shapes=[
            pltpu.VMEM((2 * reach + 2, height, depth), jnp.float32),
            pltpu.VMEM((steps, extent, rows, depth), jnp.float32),
            pltpu.SemaphoreType.DMA((2 * reach + 1,)),
        ],
        compiler_params=pltpu.CompilerParams(vmem_limit_bytes=40 * 1024 * 1024),
        name="window",
    )(meta, *mine, *theirs, got)
    end = lax.ppermute(end, axes, swap)
    parts = lax.all_to_all(grads, axes, 0, 0, axis_index_groups=pair, tiled=True)
    total = jnp.sum(parts, axis=0)
    return (end[None], total[0], total[1])


def solution(mesh):
    in_specs = (
        P("slab", None, None),
        P("slab", None, None),
        P("slab", None, None),
        P("shot", None, "slab", None, None),
        P("shot", None, "slab", None, None),
        P("shot", None),
        P("shot"),
        P("shot", None, "slab"),
        P("slab", None),
        P("slab"),
    )
    out_specs = (
        P("shot", None, "slab", None, None),
        P("slab", "shot", None),
        P("slab", "shot", None),
    )
    return jax.shard_map(shards, mesh=mesh, in_specs=in_specs, out_specs=out_specs, check_vma=False)
```

time: 157 us -> 126 us (0.80)
  the two profiles are of different devices: /device:TPU:1 before, /device:TPU:387 now
where the time goes in v2:
time: 126 us
  starting transfers between devices  50.9 us (40%)
  waiting for transfers between devices  42.8 us (34%)
  Pallas kernels  25.8 us (20%)
  local copies, waits for them, and re-layouts  4.63 us (4%)
  between operations  1.43 us (1%)
    ppermute x4, waiting for transfers between devices, shards(): mine.append(lax.ppermute(block, axes, pairs))  27.8 us
    pallas_call x1, Pallas kernels, shards(): pl.pallas_call(functools.partial(window_kernel, counts, lanes, reach, ste...  22 us
    ppermute x4, starting transfers between devices, shards(): mine.append(lax.ppermute(block, axes, pairs))  20.2 us
    all_to_all x1, starting transfers between devices, shards(): lax.all_to_all(letters, axes, 0, 0, axis_index_groups=team, tiled=True)  10.4 us
    ppermute x4, starting transfers between devices, shards(): theirs = [lax.ppermute(mine[o], axes, across) for o in range(reach)]  8.83 us
    all_to_all x1, waiting for transfers between devices, shards(): lax.all_to_all(letters, axes, 0, 0, axis_index_groups=team, tiled=True)  7.44 us
    ppermute x1, waiting for transfers between devices, shards(): end = lax.ppermute(end, axes, swap)  5.09 us
    ppermute x1, starting transfers between devices, shards(): mine = [lax.ppermute(block, axes, swap)]  4.3 us
  transfers between devices with their start and end apart: 12, of which 6 were waited for; matrix products, arithmetic and copies ran while one was open for 1% of the time, Pallas kernels for 1%

profile of v2, /device:TPU:387, one launch (start us, length us, event | category | flops | bytes accessed | tf_op | source)
XLA Modules:
  0.0 125.7 jit_solution(5803864548390771701)
XLA Ops:
  1.3 2.0 %pack.1 = f32[1360,128]{1,0:T(8,128)} custom-call(s32[1]{0:T(128)S(6)} %copy.15.cell_ref, f32[9,2,32,128]{3,2,1,0:T(8,128)} %bitcast.18, f32[9,2,32,128]{3,2,1,0:T(8,128)} %bitcast.19, f32[2,32,128]{2,1,0:T(8,128)} %lam_ref.1, f32[2,32,128]{2,1,0:T(8,128)} %mu_ref.1, f32[2,32,128]{2,1,0:T(8,128)} %buo_ref.1, f32[8,128]{1,0:T(8,128)} %bitcast.21, ...), custom_call_target="tpu_custom_call" | custom-call | tf_op jit(solution)/shard_map/pack/pallas_call | solution.py:320
  3.3 4.3 %collective-permute-start = (f32[1360,128]{1,0:T(8,128)}, f32[1360,128]{1,0:T(8,128)S(1)}, u32[]{:S(2)}, u32[]{:S(2)}) collective-permute-start(f32[1360,128]{1,0:T(8,128)} %pack.1), channel_id=1, source_target_pairs={{0,0},{1,128},{2,2},{3,130},{4,4},{5,132},{6,6},{7,134},{8,8},{9,1... | collective-permute-start | bytes 2088968 | tf_op jit(solution)/shard_map/ppermute | solution.py:338
  7.6 5.4 %collective-permute-start.4 = (f32[1360,128]{1,0:T(8,128)}, f32[1360,128]{1,0:T(8,128)S(1)}, u32[]{:S(2)}, u32[]{:S(2)}) collective-permute-start(f32[1360,128]{1,0:T(8,128)} %pack.1), channel_id=1, source_target_pairs={{5,128},{7,130},{0,4},{9,132},{2,6},{11,134},{4,8},{13,136},{6,10}... | collective-permute-start | bytes 2088968 | tf_op jit(solution)/shard_map/ppermute | solution.py:345
  13.0 2.0 %collective-permute-start.3 = (f32[1360,128]{1,0:T(8,128)}, f32[1360,128]{1,0:T(8,128)S(1)}, u32[]{:S(2)}, u32[]{:S(2)}) collective-permute-start(f32[1360,128]{1,0:T(8,128)} %pack.1), channel_id=1, source_target_pairs={{4,128},{6,130},{1,4},{8,132},{3,6},{10,134},{5,8},{12,136},{7,10}... | collective-permute-start | bytes 2088968 | tf_op jit(solution)/shard_map/ppermute | solution.py:345
  15.0 6.0 %collective-permute-start.2 = (f32[1360,128]{1,0:T(8,128)}, f32[1360,128]{1,0:T(8,128)S(1)}, u32[]{:S(2)}, u32[]{:S(2)}) collective-permute-start(f32[1360,128]{1,0:T(8,128)} %pack.1), channel_id=1, source_target_pairs={{3,128},{0,2},{5,130},{2,4},{7,132},{4,6},{9,134},{6,8},{11,136},{... | collective-permute-start | bytes 2088968 | tf_op jit(solution)/shard_map/ppermute | solution.py:345
  21.0 6.9 %collective-permute-start.1 = (f32[1360,128]{1,0:T(8,128)}, f32[1360,128]{1,0:T(8,128)S(1)}, u32[]{:S(2)}, u32[]{:S(2)}) collective-permute-start(f32[1360,128]{1,0:T(8,128)} %pack.1), channel_id=1, source_target_pairs={{2,128},{1,2},{4,130},{3,4},{6,132},{5,6},{8,134},{7,8},{10,136},{... | collective-permute-start | bytes 2088968 | tf_op jit(solution)/shard_map/ppermute | solution.py:345
  27.9 0.9 copy-done
  28.8 1.7 %letters.1 = f32[128,128]{1,0:T(8,128)} custom-call(f32[1360,128]{1,0:T(8,128)} %copy-done), custom_call_target="tpu_custom_call" | custom-call | tf_op jit(solution)/shard_map/letters/pallas_call | solution.py:347
  30.5 10.4 %all-to-all-start = ((f32[128,1,128]{2,1,0:T(1,128)}), f32[128,1,128]{2,1,0:T(1,128)S(1)}, u32[]{:S(2)}, u32[]{:S(2)}) async-start(f32[128,1,128]{2,1,0:T(1,128)} %bitcast.20), calls=%async_computation | async-start | bytes 131072 | tf_op jit(solution)/shard_map/all_to_all | solution.py:356
  40.9 11.5 %collective-permute-done.4.refs_4_ = f32[1360,128]{1,0:T(8,128)S(1)} collective-permute-done((f32[1360,128]{1,0:T(8,128)}, f32[1360,128]{1,0:T(8,128)S(1)}, u32[]{:S(2)}, u32[]{:S(2)}) %collective-permute-start.4) | collective-permute-done | bytes 696352 | tf_op jit(solution)/shard_map/ppermute | solution.py:345
  52.5 16.3 %collective-permute-done.3.refs_3_ = f32[1360,128]{1,0:T(8,128)S(1)} collective-permute-done((f32[1360,128]{1,0:T(8,128)}, f32[1360,128]{1,0:T(8,128)S(1)}, u32[]{:S(2)}, u32[]{:S(2)}) %collective-permute-start.3) | collective-permute-done | bytes 696352 | tf_op jit(solution)/shard_map/ppermute | solution.py:345
  68.8 7.4 %all-to-all-done = f32[128,1,128]{2,1,0:T(1,128)S(1)} async-done(((f32[128,1,128]{2,1,0:T(1,128)}), f32[128,1,128]{2,1,0:T(1,128)S(1)}, u32[]{:S(2)}, u32[]{:S(2)}) %all-to-all-start) | async-done | bytes 65568 | tf_op jit(solution)/shard_map/all_to_all | solution.py:356
  76.2 2.6 %collective-permute-start.5 = (f32[1360,128]{1,0:T(8,128)}, f32[1360,128]{1,0:T(8,128)S(1)}, u32[]{:S(2)}, u32[]{:S(2)}) collective-permute-start(f32[1360,128]{1,0:T(8,128)} %copy-done), channel_id=1, source_target_pairs={{0,128},{128,0},{2,130},{130,2},{4,132},{132,4},{6,134},{134,6},{8... | collective-permute-start | bytes 2088968 | tf_op jit(solution)/shard_map/ppermute | solution.py:358
  78.8 1.9 %collective-permute-start.6 = (f32[1360,128]{1,0:T(8,128)S(1)}, f32[1360,128]{1,0:T(8,128)}, u32[]{:S(2)}, u32[]{:S(2)}) collective-permute-start(f32[1360,128]{1,0:T(8,128)S(1)} %collective-permute-done.1.refs_1_), channel_id=1, source_target_pairs={{0,128},{128,0},{2,130},{130,2},{4,132},{132,4},{6,134},{134,6},{8... | collective-permute-start | bytes 2088968 | tf_op jit(solution)/shard_map/ppermute | solution.py:358
  80.7 2.4 %collective-permute-start.7 = (f32[1360,128]{1,0:T(8,128)S(1)}, f32[1360,128]{1,0:T(8,128)}, u32[]{:S(2)}, u32[]{:S(2)}) collective-permute-start(f32[1360,128]{1,0:T(8,128)S(1)} %collective-permute-done.2.refs_2_), channel_id=1, source_target_pairs={{0,128},{128,0},{2,130},{130,2},{4,132},{132,4},{6,134},{134,6},{8... | collective-permute-start | bytes 2088968 | tf_op jit(solution)/shard_map/ppermute | solution.py:358
  83.1 1.9 %collective-permute-start.8 = (f32[1360,128]{1,0:T(8,128)S(1)}, f32[1360,128]{1,0:T(8,128)}, u32[]{:S(2)}, u32[]{:S(2)}) collective-permute-start(f32[1360,128]{1,0:T(8,128)S(1)} %collective-permute-done.3.refs_3_), channel_id=1, source_target_pairs={{0,128},{128,0},{2,130},{130,2},{4,132},{132,4},{6,134},{134,6},{8... | collective-permute-start | bytes 2088968 | tf_op jit(solution)/shard_map/ppermute | solution.py:358
  85.2 2.2 %collective-permute-done.8.refs_8_ = f32[1360,128]{1,0:T(8,128)} collective-permute-done((f32[1360,128]{1,0:T(8,128)S(1)}, f32[1360,128]{1,0:T(8,128)}, u32[]{:S(2)}, u32[]{:S(2)}) %collective-permute-start.8) | collective-permute-done | bytes 696352 | tf_op jit(solution)/shard_map/ppermute | solution.py:358
  87.3 1.1 copy-done.1
  88.4 22.0 %window.1 = (f32[9,2,32,128]{3,2,1,0:T(8,128)S(1)}, f32[8,2,2,8,128]{4,3,2,1,0:T(8,128)S(1)}) custom-call(s32[2]{0:T(128)S(1)} %pad_add_fusion.meta_ref, f32[1360,128]{1,0:T(8,128)S(1)} %copy-done.1, f32[1360,128]{1,0:T(8,128)S(1)} %collective-permute-done.1.refs_1_, f32[1360,128]{1,0:T(8,128)S(1)} %collective-permute-done.2.refs_2_, ...), custom_call_target="tpu_custom_call" | custom-call | tf_op jit(solution)/shard_map/window/pallas_call | solution.py:364
  111.1 0.7 copy-done.3
  111.9 3.3 %all-to-all-start.1 = ((f32[8,2,2,8,128]{4,3,2,1,0:T(8,128)}), f32[8,2,2,8,128]{4,3,2,1,0:T(8,128)S(1)}, u32[]{:S(2)}, u32[]{:S(2)}) async-start(f32[8,2,2,8,128]{4,3,2,1,0:T(8,128)} %copy-done.2), calls=%async_computation.1 | async-start | bytes 262144 | tf_op jit(solution)/shard_map/all_to_all | solution.py:381
  115.2 3.8 %collective-permute-start.9 = (f32[9,2,32,128]{3,2,1,0:T(8,128)}, f32[9,2,32,128]{3,2,1,0:T(8,128)S(1)}, u32[]{:S(2)}, u32[]{:S(2)}) collective-permute-start(f32[9,2,32,128]{3,2,1,0:T(8,128)} %copy-done.3), channel_id=1, source_target_pairs={{0,0},{1,128},{2,2},{3,130},{4,4},{5,132},{6,6},{7,134},{8,8},{9,1... | collective-permute-start | bytes 884744 | tf_op jit(solution)/shard_map/ppermute | solution.py:380
  119.9 5.1 %collective-permute-done.9 = f32[9,2,32,128]{3,2,1,0:T(8,128)S(1)} collective-permute-done((f32[9,2,32,128]{3,2,1,0:T(8,128)}, f32[9,2,32,128]{3,2,1,0:T(8,128)S(1)}, u32[]{:S(2)}, u32[]{:S(2)}) %collective-permute-start.9) | collective-permute-done | bytes 294944 | tf_op jit(solution)/shard_map/ppermute | solution.py:380
  124.9 0.7 copy.16
  (15 shorter events, 1.6 us)
Async XLA Ops:
  3.3 24.6 %collective-permute-start = (f32[1360,128]{1,0:T(8,128)}, f32[1360,128]{1,0:T(8,128)S(1)}, u32[]{:S(2)}, u32[]{:S(2)}) collective-permute-start(f32[1360,128]{1,0:T(8,128)} %pack.1), channel_id=1, source_target_pairs={{0,0},{1,128},{2,2},{3,130},{4,4},{5,132},{6,6},{7,134},{8,8},{9,1... | collective-permute-start | bytes 2088968 | tf_op jit(solution)/shard_map/ppermute | solution.py:338
  7.6 44.9 %collective-permute-start.4 = (f32[1360,128]{1,0:T(8,128)}, f32[1360,128]{1,0:T(8,128)S(1)}, u32[]{:S(2)}, u32[]{:S(2)}) collective-permute-start(f32[1360,128]{1,0:T(8,128)} %pack.1), channel_id=1, source_target_pairs={{5,128},{7,130},{0,4},{9,132},{2,6},{11,134},{4,8},{13,136},{6,10}... | collective-permute-start | bytes 2088968 | tf_op jit(solution)/shard_map/ppermute | solution.py:345
  13.0 55.8 %collective-permute-start.3 = (f32[1360,128]{1,0:T(8,128)}, f32[1360,128]{1,0:T(8,128)S(1)}, u32[]{:S(2)}, u32[]{:S(2)}) collective-permute-start(f32[1360,128]{1,0:T(8,128)} %pack.1), channel_id=1, source_target_pairs={{4,128},{6,130},{1,4},{8,132},{3,6},{10,134},{5,8},{12,136},{7,10}... | collective-permute-start | bytes 2088968 | tf_op jit(solution)/shard_map/ppermute | solution.py:345
  15.0 53.7 %collective-permute-start.2 = (f32[1360,128]{1,0:T(8,128)}, f32[1360,128]{1,0:T(8,128)S(1)}, u32[]{:S(2)}, u32[]{:S(2)}) collective-permute-start(f32[1360,128]{1,0:T(8,128)} %pack.1), channel_id=1, source_target_pairs={{3,128},{0,2},{5,130},{2,4},{7,132},{4,6},{9,134},{6,8},{11,136},{... | collective-permute-start | bytes 2088968 | tf_op jit(solution)/shard_map/ppermute | solution.py:345
  21.0 47.8 %collective-permute-start.1 = (f32[1360,128]{1,0:T(8,128)}, f32[1360,128]{1,0:T(8,128)S(1)}, u32[]{:S(2)}, u32[]{:S(2)}) collective-permute-start(f32[1360,128]{1,0:T(8,128)} %pack.1), channel_id=1, source_target_pairs={{2,128},{1,2},{4,130},{3,4},{6,132},{5,6},{8,134},{7,8},{10,136},{... | collective-permute-start | bytes 2088968 | tf_op jit(solution)/shard_map/ppermute | solution.py:345
  27.9 0.9 copy-start
  30.5 45.7 %all-to-all-start = ((f32[128,1,128]{2,1,0:T(1,128)}), f32[128,1,128]{2,1,0:T(1,128)S(1)}, u32[]{:S(2)}, u32[]{:S(2)}) async-start(f32[128,1,128]{2,1,0:T(1,128)} %bitcast.20), calls=%async_computation | async-start | bytes 131072 | tf_op jit(solution)/shard_map/all_to_all | solution.py:356
  76.2 8.9 %collective-permute-start.5 = (f32[1360,128]{1,0:T(8,128)}, f32[1360,128]{1,0:T(8,128)S(1)}, u32[]{:S(2)}, u32[]{:S(2)}) collective-permute-start(f32[1360,128]{1,0:T(8,128)} %copy-done), channel_id=1, source_target_pairs={{0,128},{128,0},{2,130},{130,2},{4,132},{132,4},{6,134},{134,6},{8... | collective-permute-start | bytes 2088968 | tf_op jit(solution)/shard_map/ppermute | solution.py:358
  78.8 6.4 %collective-permute-start.6 = (f32[1360,128]{1,0:T(8,128)S(1)}, f32[1360,128]{1,0:T(8,128)}, u32[]{:S(2)}, u32[]{:S(2)}) collective-permute-start(f32[1360,128]{1,0:T(8,128)S(1)} %collective-permute-done.1.refs_1_), channel_id=1, source_target_pairs={{0,128},{128,0},{2,130},{130,2},{4,132},{132,4},{6,134},{134,6},{8... | collective-permute-start | bytes 2088968 | tf_op jit(solution)/shard_map/ppermute | solution.py:358
  80.7 4.4 %collective-permute-start.7 = (f32[1360,128]{1,0:T(8,128)S(1)}, f32[1360,128]{1,0:T(8,128)}, u32[]{:S(2)}, u32[]{:S(2)}) collective-permute-start(f32[1360,128]{1,0:T(8,128)S(1)} %collective-permute-done.2.refs_2_), channel_id=1, source_target_pairs={{0,128},{128,0},{2,130},{130,2},{4,132},{132,4},{6,134},{134,6},{8... | collective-permute-start | bytes 2088968 | tf_op jit(solution)/shard_map/ppermute | solution.py:358
  83.1 4.2 %collective-permute-start.8 = (f32[1360,128]{1,0:T(8,128)S(1)}, f32[1360,128]{1,0:T(8,128)}, u32[]{:S(2)}, u32[]{:S(2)}) collective-permute-start(f32[1360,128]{1,0:T(8,128)S(1)} %collective-permute-done.3.refs_3_), channel_id=1, source_target_pairs={{0,128},{128,0},{2,130},{130,2},{4,132},{132,4},{6,134},{134,6},{8... | collective-permute-start | bytes 2088968 | tf_op jit(solution)/shard_map/ppermute | solution.py:358
  87.3 1.1 copy-start.1
  110.5 0.7 copy-start.2
  111.1 0.7 copy-start.3
  111.9 7.4 %all-to-all-start.1 = ((f32[8,2,2,8,128]{4,3,2,1,0:T(8,128)}), f32[8,2,2,8,128]{4,3,2,1,0:T(8,128)S(1)}, u32[]{:S(2)}, u32[]{:S(2)}) async-start(f32[8,2,2,8,128]{4,3,2,1,0:T(8,128)} %copy-done.2), calls=%async_computation.1 | async-start | bytes 262144 | tf_op jit(solution)/shard_map/all_to_all | solution.py:381
  115.2 9.8 %collective-permute-start.9 = (f32[9,2,32,128]{3,2,1,0:T(8,128)}, f32[9,2,32,128]{3,2,1,0:T(8,128)S(1)}, u32[]{:S(2)}, u32[]{:S(2)}) collective-permute-start(f32[9,2,32,128]{3,2,1,0:T(8,128)} %copy-done.3), channel_id=1, source_target_pairs={{0,0},{1,128},{2,2},{3,130},{4,4},{5,132},{6,6},{7,134},{8,8},{9,1... | collective-permute-start | bytes 884744 | tf_op jit(solution)/shard_map/ppermute | solution.py:380

commit v3 on v2

v3 whole, which is shorter than its diff:
```python
import functools

import jax
import jax.numpy as jnp
from jax import lax
from jax.experimental import pallas as pl
from jax.experimental.pallas import tpu as pltpu
from jax.sharding import PartitionSpec as P

TIME_STEP = 0.3
CAP = 2
LANES = 128
FIELDS = 21
NOTES = 16


def reach_steps(steps, planes, reach):
    counts = {}
    for e in range(-reach, reach + 1):
        gap = planes * (abs(e) - 1) + 1 if e else 0
        counts[e] = max(0, steps - gap)
    return counts


def message_lanes(counts):
    lanes, at = {}, 0
    for e in sorted(counts, key=abs):
        for slot in range(CAP):
            lanes[e, slot] = at
            at += 1 + counts[e]
    return lanes, at


def split3(x):
    hi = x.astype(jnp.bfloat16)
    rest = x - hi.astype(jnp.float32)
    mid = rest.astype(jnp.bfloat16)
    low = (rest - mid.astype(jnp.float32)).astype(jnp.bfloat16)
    return hi, mid, low


def dot_onehot(values, onehot, dims):
    hi, mid, low = split3(values)
    hot = onehot.astype(jnp.bfloat16)
    go = lambda part: lax.dot_general(part, hot, dims, preferred_element_type=jnp.float32)
    return go(hi) + (go(mid) + go(low))


def onehot_dot(onehot, values, dims):
    hi, mid, low = split3(values)
    hot = onehot.astype(jnp.bfloat16)
    go = lambda part: lax.dot_general(hot, part, dims, preferred_element_type=jnp.float32)
    return go(hi) + (go(mid) + go(low))


def letters_kernel(counts, lanes, reach, steps, note_ref, out_ref, rows_ref):
    count = note_ref.shape[1]
    notes = note_ref[...]
    slab_row = jnp.broadcast_to(notes[steps : steps + 1], (count, count))
    slab_col = slab_row.T
    sub = lax.broadcasted_iota(jnp.int32, (count, count), 0)
    lane = lax.broadcasted_iota(jnp.int32, (count, count), 1)
    same = jnp.where((slab_col == slab_row) & (lane < sub), 1.0, 0.0)
    slot_of = jnp.sum(same, axis=1, keepdims=True)
    src = lax.broadcasted_iota(jnp.int32, (NOTES, LANES), 0)
    dst = lax.broadcasted_iota(jnp.int32, (NOTES, LANES), 1)
    spread = jnp.zeros((NOTES, LANES), jnp.float32)
    slot_lane = jnp.zeros((1, LANES), jnp.float32)
    one_lane = lax.broadcasted_iota(jnp.int32, (1, LANES), 1)
    for (e, slot), at in lanes.items():
        n = counts[e]
        spread = jnp.where((dst == at) & (src == steps + 1), 1.0, spread)
        spread = jnp.where((dst > at) & (dst <= at + n) & (src == dst - at - 1), 1.0, spread)
        slot_lane = jnp.where((one_lane >= at) & (one_lane <= at + n), float(slot), slot_lane)
    wide = dot_onehot(notes, spread, (((0,), (0,)), ((), ())))
    wide = jnp.where(slot_of == slot_lane, wide, 0.0)
    pick = jnp.where(slab_row == sub.astype(jnp.float32), 1.0, 0.0)
    rows = onehot_dot(pick, wide, (((1,), (0,)), ((), ())))
    rows_ref[...] = jnp.zeros_like(rows_ref)
    rows_ref[8 : 8 + count] = rows
    letter = jnp.zeros((count, LANES), jnp.float32)
    for e in range(-reach, reach + 1):
        start, end = lanes[e, 0], lanes[e, CAP - 1] + counts[e]
        letter = jnp.where((lane >= start) & (lane <= end), rows_ref[8 + e : 8 + e + count], letter)
    out_ref[...] = letter


def pack_kernel(cell_ref, f_ref, a_ref, lam_ref, mu_ref, buo_ref, trace_ref, slab_ref, spot_ref, wave_ref, out_ref):
    planes, rows, depth = lam_ref.shape
    one = planes * rows
    for c in range(9):
        out_ref[c * one : (c + 1) * one] = f_ref[c].reshape(one, depth)
        at = 12 * one + NOTES + c * one
        out_ref[at : at + one] = a_ref[c].reshape(one, depth)
    for c, ref in enumerate((lam_ref, mu_ref, buo_ref)):
        out_ref[(9 + c) * one : (10 + c) * one] = TIME_STEP * ref[...].reshape(one, depth)
    at, steps = 12 * one, trace_ref.shape[0]
    out_ref[at + 8 : at + NOTES] = jnp.zeros((NOTES - 8, depth), jnp.float32)
    out_ref[at : at + steps] = trace_ref[...]
    out_ref[at + steps : at + steps + 1] = slab_ref[...].astype(jnp.float32)
    out_ref[at + steps + 1 : at + steps + 2] = spot_ref[...].astype(jnp.float32)
    out_ref[at + steps + 2 : at + steps + 3, 0:steps] = wave_ref[...]
    out_ref[at + steps + 3 : at + steps + 4] = jnp.full((1, depth), cell_ref[0], jnp.int32).astype(jnp.float32)


class Window:
    def __init__(self, state, planes, rows, field, params, slab):
        self.state, self.planes, self.rows = state, planes, rows
        self.first = planes * slab
        self.one = planes * rows
        self.height = 12 * self.one + NOTES
        self.field, self.params = field, params
        self.own = pl.multiple_of(slab * self.height, 16)
        depth = state.shape[1]
        self.y = lax.broadcasted_iota(jnp.int32, (rows, depth), 0)
        self.z = lax.broadcasted_iota(jnp.int32, (rows, depth), 1)
        self.ends = (self.y == 0, self.y == rows - 1, self.z == 0, self.z == depth - 1)

    def fill(self, mine, theirs, sems, core, reach, start):
        copies = []
        for o in range(reach + 1):
            copies.append((mine[o], reach + core + (2 * core - 1) * o))
        for o in range(reach):
            copies.append((theirs[o], reach + 1 - core + (1 - 2 * core) * o))
        copies = [
            pltpu.make_async_copy(
                block.at[pl.ds(start, self.height)],
                self.state.at[pl.ds(pl.multiple_of(at * self.height, 16), self.height)],
                sems.at[i],
            )
            for i, (block, at) in enumerate(copies)
        ]
        for copy in copies:
            copy.start()
        return copies

    def base(self, p):
        return (p // self.planes) * self.height + (p % self.planes) * self.rows

    def at(self, base, row):
        return pl.ds(pl.multiple_of(self.own + (base + row), 8), self.rows)

    def get(self, base, c):
        return self.state[self.at(base, self.field + c * self.one)]

    def param(self, base, c):
        return self.state[self.at(base, self.params + c * self.one)]

    def put(self, base, values):
        for c, value in values:
            self.state[self.at(base, self.field + c * self.one)] = value

    def prev_y(self, x):
        return jnp.where(self.ends[0], 0.0, pltpu.roll(x, 1, 0))

    def next_y(self, x):
        return jnp.where(self.ends[1], 0.0, pltpu.roll(x, x.shape[0] - 1, 0))

    def prev_z(self, x):
        return jnp.where(self.ends[2], 0.0, pltpu.roll(x, 1, 1))

    def next_z(self, x):
        return jnp.where(self.ends[3], 0.0, pltpu.roll(x, x.shape[1] - 1, 1))

    def velocity(self, p, along_x=True, across=True):
        here, after, before = self.base(p), self.base(p + 1), self.base(p - 1)
        get = self.get
        factor = self.param(here, 2)
        sxy, sxz = get(here, 6), get(here, 7)
        out = []
        if along_x:
            accel = (get(after, 3) - get(here, 3)) + (sxy - self.prev_y(sxy)) + (sxz - self.prev_z(sxz))
            out.append((0, get(here, 0) - factor * accel))
        if across:
            syy, szz, syz = get(here, 4), get(here, 5), get(here, 8)
            accel = (sxy - get(before, 6)) + (self.next_y(syy) - syy) + (syz - self.prev_z(syz))
            out.append((1, get(here, 1) - factor * accel))
            accel = (sxz - get(before, 7)) + (syz - self.prev_y(syz)) + (self.next_z(szz) - szz)
            out.append((2, get(here, 2) - factor * accel))
        return here, out

    def stress(self, p, push=None):
        here, after, before = self.base(p), self.base(p + 1), self.base(p - 1)
        get = self.get
        lam, mu = self.param(here, 0), self.param(here, 1)
        twice = 2.0 * mu
        vx, vy, vz = get(here, 0), get(here, 1), get(here, 2)
        exx = vx - get(before, 0)
        eyy = vy - self.prev_y(vy)
        ezz = vz - self.prev_z(vz)
        exy = (self.next_y(vx) - vx) + (get(after, 1) - vy)
        exz = (self.next_z(vx) - vx) + (get(after, 2) - vz)
        eyz = (self.next_z(vy) - vy) + (self.next_y(vz) - vz)
        volume = lam * (exx + eyy + ezz)
        if push is not None:
            volume = volume + push
        out = [
            (3, get(here, 3) - (volume + twice * exx)),
            (4, get(here, 4) - (volume + twice * eyy)),
            (5, get(here, 5) - (volume + twice * ezz)),
            (6, get(here, 6) - mu * exy),
            (7, get(here, 7) - mu * exz),
            (8, get(here, 8) - mu * eyz),
        ]
        return here, out, (exx, eyy, ezz, exy, exz, eyz)

    def step(self, k, steps, push, see):
        m = steps - 1 - k
        low, high = -m, self.planes + m
        pushed = lambda p: None if push is None else push[k, self.first + p]
        ready = []
        for p in range(low - 1, high + 1):
            ready.append(self.velocity(p, along_x=p < high, across=p >= low))
            if p >= low:
                self.put(*ready.pop(0))
        self.put(*ready.pop(0))
        for p in range(low, high):
            here, out, strains = self.stress(p, pushed(p))
            self.put(here, out)
            if 0 <= p < self.planes:
                see(k, p, strains)


def forward_kernel(reach, steps, planes, rows, meta_ref, *refs):
    mine, theirs = refs[: reach + 1], refs[reach + 1 : 2 * reach + 1]
    strain_ref, state, sems = refs[2 * reach + 1 :]
    depth = state.shape[1]
    one = planes * rows
    core, slab = meta_ref[0], meta_ref[1]
    window = Window(state, planes, rows, 0, 9 * one, reach + core)
    for copy in window.fill(mine, theirs, sems, core, reach, 0):
        copy.wait()
    halo = planes * (reach + core)
    at = pl.multiple_of((reach + core) * window.height + 12 * one + steps, 8)
    notes = state[pl.ds(at, 8)]
    wave, cell = notes[2:3], jnp.max(notes[3:4]).astype(jnp.int32)
    src_plane = cell // (rows * depth) - planes * slab
    spot = jnp.where(window.y * depth + window.z == cell % (rows * depth), TIME_STEP, 0.0)

    def see(k, p, strains):
        for c, strain in enumerate(strains):
            strain_ref[k, c, p] = strain

    for k in range(steps):
        window.step(k, steps, None, see)
        m = steps - 1 - k

        @pl.when((src_plane >= -m) & (src_plane < planes + m))
        def _():
            shot = wave[:, k : k + 1] * spot
            there = window.base(src_plane + planes * reach) - reach * window.height
            window.put(there, [(c, window.get(there, c) - shot) for c in (3, 4, 5)])


def adjoint_kernel(counts, lanes, reach, steps, planes, rows, meta_ref, *refs):
    mine, theirs = refs[: reach + 1], refs[reach + 1 : 2 * reach + 1]
    letters_ref, strain_ref, end_ref, grad_ref, state, push, sems = refs[2 * reach + 1 :]
    depth = state.shape[1]
    one = planes * rows
    core = meta_ref[0]
    window = Window(state, planes, rows, 3 * one + NOTES, 0, reach + core)
    copies = window.fill(mine, theirs, sems, core, reach, 9 * one)
    halo = planes * (reach + core)
    letters = letters_ref[...]
    letters_t = letters.T
    sources = letters.shape[0]
    lane_iota = lax.broadcasted_iota(jnp.int32, (sources, depth), 1)
    row_iota = lax.broadcasted_iota(jnp.int32, (one, sources), 0)
    for e in range(-reach, reach + 1):
        n = counts[e]
        lefts, rights = [], []
        for slot in range(CAP):
            at = lanes[e, slot]
            cell_col = letters[:, at : at + 1].astype(jnp.int32)
            rights.append(jnp.where(lane_iota == (cell_col & (depth - 1)), 1.0, 0.0))
            cell_row = letters_t[at : at + 1, :].astype(jnp.int32) // depth
            hit = row_iota == cell_row
            lefts.append(
                jnp.concatenate([jnp.where(hit, letters_t[at + 1 + k : at + 2 + k, :], 0.0) for k in range(n)], axis=0)
            )
        left = jnp.concatenate(lefts, axis=1)
        right = jnp.concatenate(rights, axis=0)
        sums = TIME_STEP * dot_onehot(left, right, (((1,), (0,)), ((), ())))
        for k in range(n):
            push[k, pl.ds(halo + planes * e, planes)] = sums[k * one : (k + 1) * one].reshape(planes, rows, depth)
    for copy in copies:
        copy.wait()

    totals = [[jnp.zeros((rows, depth), jnp.float32)] * 2 for _ in range(planes)]

    def see(k, p, strains):
        axx, ayy, azz, axy, axz, ayz = (strain_ref[k, c, p] for c in range(6))
        bxx, byy, bzz, bxy, bxz, byz = strains
        first = (axx + ayy + azz) * (bxx + byy + bzz)
        second = 2.0 * (axx * bxx + ayy * byy + azz * bzz) + axy * bxy + axz * bxz + ayz * byz
        totals[p] = [totals[p][0] + first, totals[p][1] + second]

    for k in range(steps):
        window.step(k, steps, push, see)

    own = pl.multiple_of((reach + core) * window.height + window.field, 16)
    final = pltpu.make_async_copy(state.at[pl.ds(own, 9 * one)], end_ref, sems.at[2 * reach + 1])
    final.start()
    shots = grad_ref.shape[0] // 2
    share = rows // shots
    for p in range(planes):
        for g in range(2):
            total = TIME_STEP * totals[p][g]
            for j in range(shots):
                for h in range(2):
                    grad_ref[2 * j + h, g, p] = jnp.where(core == h, total[j * share : (j + 1) * share], 0.0)
    final.wait()


def vmem():
    return pl.BlockSpec(memory_space=pltpu.VMEM)


def smem():
    return pl.BlockSpec(memory_space=pltpu.SMEM)


def hbm():
    return pl.BlockSpec(memory_space=pltpu.HBM)


def shards(
    lame_lambda,
    lame_mu,
    buoyancy,
    forward_state,
    adjoint_state,
    source_wavelet,
    source_cell,
    residual_traces,
    receiver_slab,
    receiver_cell,
):
    planes, rows, depth = lame_lambda.shape
    one = planes * rows
    steps = source_wavelet.shape[1]
    slabs = lax.axis_size("slab")
    shots = lax.axis_size("shot")
    axes = ("shot", "slab")
    reach = -(-steps // planes)
    counts = reach_steps(steps, planes, reach)
    lanes, _ = message_lanes(counts)
    height = FIELDS * one + NOTES

    def at(s, d):
        return ((s & ~1) | (d & 1)) * slabs + ((d & ~1) | (s & 1))

    every = [(s, d) for s in range(shots) for d in range(slabs)]
    swap = [(s * slabs + d, at(s, d)) for s, d in every]
    across = [(at(s, d), at(s, d ^ 1)) for s, d in every]
    team = [[at(s, d) for d in range(slabs)] for s in range(shots)]
    pair = [[s * slabs + 2 * q + h for s in range(shots) for h in range(2)] for q in range(slabs // 2)]

    block = pl.pallas_call(
        pack_kernel,
        out_shape=jax.ShapeDtypeStruct((height, depth), jnp.float32),
        in_specs=[smem()] + [vmem()] * 9,
        out_specs=vmem(),
        name="pack",
    )(
        source_cell,
        forward_state[0],
        adjoint_state[0],
        lame_lambda,
        lame_mu,
        buoyancy,
        residual_traces[0],
        receiver_slab.reshape(1, -1),
        receiver_cell.reshape(1, -1),
        source_wavelet,
    )
    mine = [lax.ppermute(block, axes, swap)]
    for o in range(1, reach + 1):
        pairs = []
        for s, d in every:
            i = d + o if d % 2 else d - o
            if 0 <= i < slabs:
                pairs.append((s * slabs + i, at(s, d)))
        mine.append(lax.ppermute(block, axes, pairs))

    letters = pl.pallas_call(
        functools.partial(letters_kernel, counts, lanes, reach, steps),
        grid=(1,),
        out_shape=jax.ShapeDtypeStruct((slabs, LANES), jnp.float32),
        in_specs=[pl.BlockSpec((NOTES, depth), lambda i: (12 * one // NOTES, 0))],
        out_specs=pl.BlockSpec((slabs, LANES), lambda i: (0, 0)),
        scratch_shapes=[pltpu.VMEM((slabs + 16, LANES), jnp.float32)],
        name="letters",
    )(mine[0])
    got = lax.all_to_all(letters, axes, 0, 0, axis_index_groups=team, tiled=True)
    my_shot, my_slab = lax.axis_index("shot"), lax.axis_index("slab")
    core = my_shot & 1
    meta = jnp.stack([core, (my_slab & ~1) | core]).astype(jnp.int32)
    extent = planes * (2 * reach + 2)
    held = pltpu.VMEM(((2 * reach + 2) * (12 * one + NOTES), depth), jnp.float32)
    cost = pl.CostEstimate(flops=60_000_000, transcendentals=0, bytes_accessed=16_000_000)

    def share_and_run(mine):
        theirs = [lax.ppermute(mine[o], axes, across) for o in range(reach)]
        strains = pl.pallas_call(
            functools.partial(forward_kernel, reach, steps, planes, rows),
            out_shape=jax.ShapeDtypeStruct((steps, 6, planes, rows, depth), jnp.float32),
            in_specs=[smem()] + [hbm()] * (2 * reach + 1),
            out_specs=vmem(),
            scratch_shapes=[held, pltpu.SemaphoreType.DMA((2 * reach + 1,))],
            compiler_params=pltpu.CompilerParams(vmem_limit_bytes=60 * 1024 * 1024),
            cost_estimate=cost,
            name="forward",
        )(meta, *mine, *theirs)
        return (*theirs, strains)

    def nothing(mine):
        return (*mine[:reach], jnp.zeros((steps, 6, planes, rows, depth), jnp.float32))

    *theirs, strains = lax.cond(my_slab < slabs, share_and_run, nothing, mine)
    end, grads = pl.pallas_call(
        functools.partial(adjoint_kernel, counts, lanes, reach, steps, planes, rows),
        out_shape=(
            jax.ShapeDtypeStruct((9 * one, depth), jnp.float32),
            jax.ShapeDtypeStruct((2 * shots, 2, planes, rows // shots, depth), jnp.float32),
        ),
        in_specs=[smem()] + [hbm()] * (2 * reach + 1) + [vmem()] * 2,
        out_specs=(hbm(), vmem()),
        scratch_shapes=[
            held,
            pltpu.VMEM((steps, extent, rows, depth), jnp.float32),
            pltpu.SemaphoreType.DMA((2 * reach + 2,)),
        ],
        compiler_params=pltpu.CompilerParams(vmem_limit_bytes=60 * 1024 * 1024),
        cost_estimate=cost,
        name="adjoint",
    )(meta, *mine, *theirs, got, strains)
    end = lax.ppermute(end, axes, swap)
    parts = lax.all_to_all(grads, axes, 0, 0, axis_index_groups=pair, tiled=True)
    total = jnp.sum(parts, axis=0)
    return (end.reshape(1, 9, planes, rows, depth), total[0], total[1])


def solution(mesh):
    in_specs = (
        P("slab", None, None),
        P("slab", None, None),
        P("slab", None, None),
        P("shot", None, "slab", None, None),
        P("shot", None, "slab", None, None),
        P("shot", None),
        P("shot"),
        P("shot", None, "slab"),
        P("slab", None),
        P("slab"),
    )
    out_specs = (
        P("shot", None, "slab", None, None),
        P("slab", "shot", None),
        P("slab", "shot", None),
    )
    return jax.shard_map(shards, mesh=mesh, in_specs=in_specs, out_specs=out_specs, check_vma=False)
```

time: 126 us -> 113 us (0.90)
  the two profiles are of different devices: /device:TPU:387 before, /device:TPU:163 now
where the time goes in v3:
time: 113 us; the launch traced here: 112 us
  starting transfers between devices  55.2 us (49%)
  waiting for transfers between devices  34.6 us (31%)
  Pallas kernels  17.9 us (16%)
  local copies, waits for them, and re-layouts  2.82 us (2%)
  between operations  1.4 us (1%)
    ppermute x4, waiting for transfers between devices, shards(): mine.append(lax.ppermute(block, axes, pairs))  27 us
    all_to_all x1, starting transfers between devices, shards(): lax.all_to_all(letters, axes, 0, 0, axis_index_groups=team, tiled=True)  18.1 us
    ppermute x4, starting transfers between devices, shards(): mine.append(lax.ppermute(block, axes, pairs))  17.2 us
    ppermute x4, starting transfers between devices, share_and_run(): theirs = [lax.ppermute(mine[o], axes, across) for o in range(reach)]  8.65 us
    pallas_call x1, Pallas kernels, shards(): pl.pallas_call(functools.partial(adjoint_kernel, counts, lanes, reach, st...  8.5 us
    pallas_call x1, Pallas kernels, share_and_run(): pl.pallas_call(functools.partial(forward_kernel, reach, steps, planes, ro...  6.36 us
    ppermute x1, waiting for transfers between devices, shards(): end = lax.ppermute(end, axes, swap)  5.24 us
    ppermute x1, starting transfers between devices, shards(): mine = [lax.ppermute(block, axes, swap)]  4.3 us
  transfers between devices with their start and end apart: 12, of which 6 were waited for; matrix products, arithmetic and copies ran while one was open for 1% of the time, Pallas kernels for 7%

profile of v3, /device:TPU:163, one launch (start us, length us, event | category | flops | bytes accessed | tf_op | source)
XLA Modules:
  0.0 112.1 jit_solution(12249068161332333591)
XLA Ops:
  1.3 2.0 %pack.1 = f32[1360,128]{1,0:T(8,128)} custom-call(s32[1]{0:T(128)S(6)} %copy.25.cell_ref, f32[9,2,32,128]{3,2,1,0:T(8,128)} %bitcast.17, f32[9,2,32,128]{3,2,1,0:T(8,128)} %bitcast.18, f32[2,32,128]{2,1,0:T(8,128)} %lam_ref.1, f32[2,32,128]{2,1,0:T(8,128)} %mu_ref.1, f32[2,32,128]{2,1,0:T(8,128)} %buo_ref.1, f32[8,128]{1,0:T(8,128)} %bitcast.21, ...), custom_call_target="tpu_custom_call" | custom-call | tf_op jit(solution)/shard_map/pack/pallas_call | solution.py:359
  3.3 4.3 %collective-permute-start.4 = (f32[1360,128]{1,0:T(8,128)}, f32[1360,128]{1,0:T(8,128)S(1)}, u32[]{:S(2)}, u32[]{:S(2)}) collective-permute-start(f32[1360,128]{1,0:T(8,128)} %pack.1), channel_id=1, source_target_pairs={{0,0},{1,128},{2,2},{3,130},{4,4},{5,132},{6,6},{7,134},{8,8},{9,1... | collective-permute-start | bytes 2088968 | tf_op jit(solution)/shard_map/ppermute | solution.py:377
  7.6 3.2 %collective-permute-start.5 = (f32[1360,128]{1,0:T(8,128)}, f32[1360,128]{1,0:T(8,128)S(1)}, u32[]{:S(2)}, u32[]{:S(2)}) collective-permute-start(f32[1360,128]{1,0:T(8,128)} %pack.1), channel_id=1, source_target_pairs={{2,128},{1,2},{4,130},{3,4},{6,132},{5,6},{8,134},{7,8},{10,136},{... | collective-permute-start | bytes 2088968 | tf_op jit(solution)/shard_map/ppermute | solution.py:384
  10.8 3.9 %collective-permute-start.6 = (f32[1360,128]{1,0:T(8,128)}, f32[1360,128]{1,0:T(8,128)}, u32[]{:S(2)}, u32[]{:S(2)}) collective-permute-start(f32[1360,128]{1,0:T(8,128)} %pack.1), channel_id=1, source_target_pairs={{3,128},{0,2},{5,130},{2,4},{7,132},{4,6},{9,134},{6,8},{11,136},{... | collective-permute-start | bytes 2088968 | tf_op jit(solution)/shard_map/ppermute | solution.py:384
  14.7 3.1 %collective-permute-start.7 = (f32[1360,128]{1,0:T(8,128)}, f32[1360,128]{1,0:T(8,128)}, u32[]{:S(2)}, u32[]{:S(2)}) collective-permute-start(f32[1360,128]{1,0:T(8,128)} %pack.1), channel_id=1, source_target_pairs={{4,128},{6,130},{1,4},{8,132},{3,6},{10,134},{5,8},{12,136},{7,10}... | collective-permute-start | bytes 2088968 | tf_op jit(solution)/shard_map/ppermute | solution.py:384
  17.9 7.0 %collective-permute-start.8 = (f32[1360,128]{1,0:T(8,128)}, f32[1360,128]{1,0:T(8,128)S(1)}, u32[]{:S(2)}, u32[]{:S(2)}) collective-permute-start(f32[1360,128]{1,0:T(8,128)} %pack.1), channel_id=1, source_target_pairs={{5,128},{7,130},{0,4},{9,132},{2,6},{11,134},{4,8},{13,136},{6,10}... | collective-permute-start | bytes 2088968 | tf_op jit(solution)/shard_map/ppermute | solution.py:384
  24.9 1.0 letters.1
  25.9 18.1 %all-to-all-start = ((f32[128,1,128]{2,1,0:T(1,128)}), f32[128,1,128]{2,1,0:T(1,128)S(1)}, u32[]{:S(2)}, u32[]{:S(2)}) async-start(f32[128,1,128]{2,1,0:T(1,128)} %bitcast.20), calls=%async_computation | async-start | bytes 131072 | tf_op jit(solution)/shard_map/all_to_all | solution.py:395
  44.1 1.4 %collective-permute-done.6.refs_2_ = f32[1360,128]{1,0:T(8,128)} collective-permute-done((f32[1360,128]{1,0:T(8,128)}, f32[1360,128]{1,0:T(8,128)}, u32[]{:S(2)}, u32[]{:S(2)}) %collective-permute-start.6) | collective-permute-done | bytes 696352 | tf_op jit(solution)/shard_map/ppermute | solution.py:384
  45.4 10.9 %collective-permute-done.7.refs_3_ = f32[1360,128]{1,0:T(8,128)} collective-permute-done((f32[1360,128]{1,0:T(8,128)}, f32[1360,128]{1,0:T(8,128)}, u32[]{:S(2)}, u32[]{:S(2)}) %collective-permute-start.7) | collective-permute-done | bytes 696352 | tf_op jit(solution)/shard_map/ppermute | solution.py:384
  56.3 14.8 %collective-permute-done.8.refs_4_ = f32[1360,128]{1,0:T(8,128)S(1)} collective-permute-done((f32[1360,128]{1,0:T(8,128)}, f32[1360,128]{1,0:T(8,128)S(1)}, u32[]{:S(2)}, u32[]{:S(2)}) %collective-permute-start.8) | collective-permute-done | bytes 696352 | tf_op jit(solution)/shard_map/ppermute | solution.py:384
  71.1 0.9 copy-done
  72.0 17.1 %conditional.1 = (f32[1360,128]{1,0:T(8,128)}, f32[1360,128]{1,0:T(8,128)}, f32[1360,128]{1,0:T(8,128)}, f32[1360,128]{1,0:T(8,128)}, f32[8,6,2,32,128]{4,3,2,1,0:T(8,128)S(1)}) conditional(s32[]{:T(128)} %convert_element_type.3, (f32[1360,128]{1,0:T(8,128)S(1)}, f32[1360,128]{1,0:T(8,128)S(1)}, f32[1360,128]{1,0:T(8,128)}, ...), branch_computations={%region_0.0_spmd, %region_1.0_spmd} | conditional | flops 60000000 | bytes 29926628 | solution.py:420
  72.0 1.9 %collective-permute-start = (f32[1360,128]{1,0:T(8,128)S(1)}, f32[1360,128]{1,0:T(8,128)}, u32[]{:S(2)}, u32[]{:S(2)}) collective-permute-start(f32[1360,128]{1,0:T(8,128)S(1)} %get-tuple-element.24.refs_0_), channel_id=1, source_target_pairs={{0,128},{128,0},{2,130},{130,2},{4,132},{132,4},{6,134},{134,6},{8... | collective-permute-start | bytes 2088968 | tf_op jit(solution)/shard_map/cond/branch_1_fun/ppermute | solution.py:404
  73.9 2.4 %collective-permute-start.1 = (f32[1360,128]{1,0:T(8,128)S(1)}, f32[1360,128]{1,0:T(8,128)}, u32[]{:S(2)}, u32[]{:S(2)}) collective-permute-start(f32[1360,128]{1,0:T(8,128)S(1)} %get-tuple-element.25.refs_1_), channel_id=1, source_target_pairs={{0,128},{128,0},{2,130},{130,2},{4,132},{132,4},{6,134},{134,6},{8... | collective-permute-start | bytes 2088968 | tf_op jit(solution)/shard_map/cond/branch_1_fun/ppermute | solution.py:404
  76.3 1.9 %collective-permute-start.2 = (f32[1360,128]{1,0:T(8,128)}, f32[1360,128]{1,0:T(8,128)}, u32[]{:S(2)}, u32[]{:S(2)}) collective-permute-start(f32[1360,128]{1,0:T(8,128)} %get-tuple-element.26.refs_2_), channel_id=1, source_target_pairs={{0,128},{128,0},{2,130},{130,2},{4,132},{132,4},{6,134},{134,6},{8... | collective-permute-start | bytes 2088968 | tf_op jit(solution)/shard_map/cond/branch_1_fun/ppermute | solution.py:404
  78.2 2.4 %collective-permute-start.3 = (f32[1360,128]{1,0:T(8,128)}, f32[1360,128]{1,0:T(8,128)}, u32[]{:S(2)}, u32[]{:S(2)}) collective-permute-start(f32[1360,128]{1,0:T(8,128)} %get-tuple-element.27.refs_3_), channel_id=1, source_target_pairs={{0,128},{128,0},{2,130},{130,2},{4,132},{132,4},{6,134},{134,6},{8... | collective-permute-start | bytes 2088968 | tf_op jit(solution)/shard_map/cond/branch_1_fun/ppermute | solution.py:404
  80.7 2.1 %collective-permute-done.3.refs_8_ = f32[1360,128]{1,0:T(8,128)} collective-permute-done((f32[1360,128]{1,0:T(8,128)}, f32[1360,128]{1,0:T(8,128)}, u32[]{:S(2)}, u32[]{:S(2)}) %collective-permute-start.3) | collective-permute-done | bytes 696352 | tf_op jit(solution)/shard_map/cond/branch_1_fun/ppermute | solution.py:404
  82.7 6.4 %forward.1 = f32[8,6,2,32,128]{4,3,2,1,0:T(8,128)S(1)} custom-call(s32[2]{0:T(128)S(1)} %get-tuple-element.28.meta_ref, f32[1360,128]{1,0:T(8,128)S(1)} %get-tuple-element.24.refs_0_, f32[1360,128]{1,0:T(8,128)S(1)} %get-tuple-element.25.refs_1_, f32[1360,128]{1,0:T(8,128)} %get-tuple-element.26.refs_2_, f32[1360,128]{1,0:T(8,128)} %get-tuple-element.27.refs_3_, ...), custom_call_target="tpu_custom_call" | custom-call | flops 60000000 | bytes 16000000 | tf_op jit(solution)/shard_map/cond/branch_1_fun/forward/pallas_call | solution.py:405
  89.7 8.5 %adjoint.1 = (f32[576,128]{1,0:T(8,128)}, f32[8,2,2,8,128]{4,3,2,1,0:T(8,128)}) custom-call(s32[2]{0:T(128)S(1)} %pad_add_fusion.meta_ref, f32[1360,128]{1,0:T(8,128)S(1)} %collective-permute-done.4.note_ref.refs_0_, f32[1360,128]{1,0:T(8,128)S(1)} %collective-permute-done.5.refs_1_, f32[1360,128]{1,0:T(8,128)} %collective-permute-done.6.refs_2_, ...), custom_call_target="tpu_custom_call" | custom-call | flops 60000000 | bytes 16000000 | tf_op jit(solution)/shard_map/adjoint/pallas_call | solution.py:421
  98.3 3.3 %all-to-all-start.1 = ((f32[8,2,2,8,128]{4,3,2,1,0:T(8,128)}), f32[8,2,2,8,128]{4,3,2,1,0:T(8,128)S(1)}, u32[]{:S(2)}, u32[]{:S(2)}) async-start(f32[8,2,2,8,128]{4,3,2,1,0:T(8,128)} %get-tuple-element.46), calls=%async_computation.1 | async-start | bytes 262144 | tf_op jit(solution)/shard_map/all_to_all | solution.py:439
  101.6 3.7 %collective-permute-start.9 = (f32[576,128]{1,0:T(8,128)}, f32[576,128]{1,0:T(8,128)S(1)}, u32[]{:S(2)}, u32[]{:S(2)}) collective-permute-start(f32[576,128]{1,0:T(8,128)} %get-tuple-element.45), channel_id=1, source_target_pairs={{0,0},{1,128},{2,2},{3,130},{4,4},{5,132},{6,6},{7,134},{8,8},{9,1... | collective-permute-start | bytes 884744 | tf_op jit(solution)/shard_map/ppermute | solution.py:438
  106.1 5.2 %collective-permute-done.9 = f32[576,128]{1,0:T(8,128)S(1)} collective-permute-done((f32[576,128]{1,0:T(8,128)}, f32[576,128]{1,0:T(8,128)S(1)}, u32[]{:S(2)}, u32[]{:S(2)}) %collective-permute-start.9) | collective-permute-done | bytes 294944 | tf_op jit(solution)/shard_map/ppermute | solution.py:438
  111.4 0.7 copy.26
  (15 shorter events, 1.6 us)
Async XLA Ops:
  3.3 21.6 %collective-permute-start.4 = (f32[1360,128]{1,0:T(8,128)}, f32[1360,128]{1,0:T(8,128)S(1)}, u32[]{:S(2)}, u32[]{:S(2)}) collective-permute-start(f32[1360,128]{1,0:T(8,128)} %pack.1), channel_id=1, source_target_pairs={{0,0},{1,128},{2,2},{3,130},{4,4},{5,132},{6,6},{7,134},{8,8},{9,1... | collective-permute-start | bytes 2088968 | tf_op jit(solution)/shard_map/ppermute | solution.py:377
  7.6 36.5 %collective-permute-start.5 = (f32[1360,128]{1,0:T(8,128)}, f32[1360,128]{1,0:T(8,128)S(1)}, u32[]{:S(2)}, u32[]{:S(2)}) collective-permute-start(f32[1360,128]{1,0:T(8,128)} %pack.1), channel_id=1, source_target_pairs={{2,128},{1,2},{4,130},{3,4},{6,132},{5,6},{8,134},{7,8},{10,136},{... | collective-permute-start | bytes 2088968 | tf_op jit(solution)/shard_map/ppermute | solution.py:384
  10.8 34.6 %collective-permute-start.6 = (f32[1360,128]{1,0:T(8,128)}, f32[1360,128]{1,0:T(8,128)}, u32[]{:S(2)}, u32[]{:S(2)}) collective-permute-start(f32[1360,128]{1,0:T(8,128)} %pack.1), channel_id=1, source_target_pairs={{3,128},{0,2},{5,130},{2,4},{7,132},{4,6},{9,134},{6,8},{11,136},{... | collective-permute-start | bytes 2088968 | tf_op jit(solution)/shard_map/ppermute | solution.py:384
  14.7 41.6 %collective-permute-start.7 = (f32[1360,128]{1,0:T(8,128)}, f32[1360,128]{1,0:T(8,128)}, u32[]{:S(2)}, u32[]{:S(2)}) collective-permute-start(f32[1360,128]{1,0:T(8,128)} %pack.1), channel_id=1, source_target_pairs={{4,128},{6,130},{1,4},{8,132},{3,6},{10,134},{5,8},{12,136},{7,10}... | collective-permute-start | bytes 2088968 | tf_op jit(solution)/shard_map/ppermute | solution.py:384
  17.9 53.2 %collective-permute-start.8 = (f32[1360,128]{1,0:T(8,128)}, f32[1360,128]{1,0:T(8,128)S(1)}, u32[]{:S(2)}, u32[]{:S(2)}) collective-permute-start(f32[1360,128]{1,0:T(8,128)} %pack.1), channel_id=1, source_target_pairs={{5,128},{7,130},{0,4},{9,132},{2,6},{11,134},{4,8},{13,136},{6,10}... | collective-permute-start | bytes 2088968 | tf_op jit(solution)/shard_map/ppermute | solution.py:384
  25.9 63.2 %all-to-all-start = ((f32[128,1,128]{2,1,0:T(1,128)}), f32[128,1,128]{2,1,0:T(1,128)S(1)}, u32[]{:S(2)}, u32[]{:S(2)}) async-start(f32[128,1,128]{2,1,0:T(1,128)} %bitcast.20), calls=%async_computation | async-start | bytes 131072 | tf_op jit(solution)/shard_map/all_to_all | solution.py:395
  71.1 0.9 copy-start
  72.0 10.8 %copy-start.1 = (f32[1360,128]{1,0:T(8,128)}, f32[1360,128]{1,0:T(8,128)S(1)}, u32[]{:S(2)}) copy-start(f32[1360,128]{1,0:T(8,128)S(1)} %get-tuple-element.29.refs_4_) | copy-start | bytes 2088964 | tf_op jit(solution)/shard_map/cond
  72.0 8.7 %collective-permute-start = (f32[1360,128]{1,0:T(8,128)S(1)}, f32[1360,128]{1,0:T(8,128)}, u32[]{:S(2)}, u32[]{:S(2)}) collective-permute-start(f32[1360,128]{1,0:T(8,128)S(1)} %get-tuple-element.24.refs_0_), channel_id=1, source_target_pairs={{0,128},{128,0},{2,130},{130,2},{4,132},{132,4},{6,134},{134,6},{8... | collective-permute-start | bytes 2088968 | tf_op jit(solution)/shard_map/cond/branch_1_fun/ppermute | solution.py:404
  73.9 6.8 %collective-permute-start.1 = (f32[1360,128]{1,0:T(8,128)S(1)}, f32[1360,128]{1,0:T(8,128)}, u32[]{:S(2)}, u32[]{:S(2)}) collective-permute-start(f32[1360,128]{1,0:T(8,128)S(1)} %get-tuple-element.25.refs_1_), channel_id=1, source_target_pairs={{0,128},{128,0},{2,130},{130,2},{4,132},{132,4},{6,134},{134,6},{8... | collective-permute-start | bytes 2088968 | tf_op jit(solution)/shard_map/cond/branch_1_fun/ppermute | solution.py:404
  76.3 4.4 %collective-permute-start.2 = (f32[1360,128]{1,0:T(8,128)}, f32[1360,128]{1,0:T(8,128)}, u32[]{:S(2)}, u32[]{:S(2)}) collective-permute-start(f32[1360,128]{1,0:T(8,128)} %get-tuple-element.26.refs_2_), channel_id=1, source_target_pairs={{0,128},{128,0},{2,130},{130,2},{4,132},{132,4},{6,134},{134,6},{8... | collective-permute-start | bytes 2088968 | tf_op jit(solution)/shard_map/cond/branch_1_fun/ppermute | solution.py:404
  78.2 4.5 %collective-permute-start.3 = (f32[1360,128]{1,0:T(8,128)}, f32[1360,128]{1,0:T(8,128)}, u32[]{:S(2)}, u32[]{:S(2)}) collective-permute-start(f32[1360,128]{1,0:T(8,128)} %get-tuple-element.27.refs_3_), channel_id=1, source_target_pairs={{0,128},{128,0},{2,130},{130,2},{4,132},{132,4},{6,134},{134,6},{8... | collective-permute-start | bytes 2088968 | tf_op jit(solution)/shard_map/cond/branch_1_fun/ppermute | solution.py:404
  89.1 0.6 copy-start.2
  98.3 7.2 %all-to-all-start.1 = ((f32[8,2,2,8,128]{4,3,2,1,0:T(8,128)}), f32[8,2,2,8,128]{4,3,2,1,0:T(8,128)S(1)}, u32[]{:S(2)}, u32[]{:S(2)}) async-start(f32[8,2,2,8,128]{4,3,2,1,0:T(8,128)} %get-tuple-element.46), calls=%async_computation.1 | async-start | bytes 262144 | tf_op jit(solution)/shard_map/all_to_all | solution.py:439
  101.6 9.8 %collective-permute-start.9 = (f32[576,128]{1,0:T(8,128)}, f32[576,128]{1,0:T(8,128)S(1)}, u32[]{:S(2)}, u32[]{:S(2)}) collective-permute-start(f32[576,128]{1,0:T(8,128)} %get-tuple-element.45), channel_id=1, source_target_pairs={{0,0},{1,128},{2,2},{3,130},{4,4},{5,132},{6,6},{7,134},{8,8},{9,1... | collective-permute-start | bytes 884744 | tf_op jit(solution)/shard_map/ppermute | solution.py:438

commit v4 on v3

--- a/solution.py
+++ b/solution.py
@@ -400,8 +400,16 @@
     held = pltpu.VMEM(((2 * reach + 2) * (12 * one + NOTES), depth), jnp.float32)
     cost = pl.CostEstimate(flops=60_000_000, transcendentals=0, bytes_accessed=16_000_000)
 
-    def share_and_run(mine):
-        theirs = [lax.ppermute(mine[o], axes, across) for o in range(reach)]
+    def share(blocks):
+        return [lax.ppermute(block, axes, across) for block in blocks]
+
+    here = my_slab < slabs
+    theirs = []
+    theirs += lax.cond(here, share, lambda blocks: blocks, mine[0:2])
+    theirs += lax.cond(here, share, lambda blocks: blocks, mine[2:3])
+    theirs += lax.cond(here, share, lambda blocks: blocks, mine[3:reach])
+
+    def run(blocks):
         strains = pl.pallas_call(
             functools.partial(forward_kernel, reach, steps, planes, rows),
             out_shape=jax.ShapeDtypeStruct((steps, 6, planes, rows, depth), jnp.float32),
@@ -411,13 +419,10 @@
             compiler_params=pltpu.CompilerParams(vmem_limit_bytes=60 * 1024 * 1024),
             cost_estimate=cost,
             name="forward",
-        )(meta, *mine, *theirs)
-        return (*theirs, strains)
-
-    def nothing(mine):
-        return (*mine[:reach], jnp.zeros((steps, 6, planes, rows, depth), jnp.float32))
-
-    *theirs, strains = lax.cond(my_slab < slabs, share_and_run, nothing, mine)
+        )(meta, *blocks)
+        return strains
+
+    strains = lax.cond(here, run, lambda blocks: jnp.zeros((steps, 6, planes, rows, depth), jnp.float32), (*mine, *theirs))
     end, grads = pl.pallas_call(
         functools.partial(adjoint_kernel, counts, lanes, reach, steps, planes, rows),
         out_shape=(

time: 113 us -> 103 us (0.912)
  the two profiles are of different devices: /device:TPU:163 before, /device:TPU:1 now
where the time goes in v4:
time: 103 us; the launch traced here: 102 us
  starting transfers between devices  68.5 us (67%)
  Pallas kernels  17.9 us (17%)
  waiting for transfers between devices  10.8 us (10%)
  local copies, waits for them, and re-layouts  2.81 us (3%)
  between operations  1.39 us (1%)
    all_to_all x1, starting transfers between devices, shards(): lax.all_to_all(letters, axes, 0, 0, axis_index_groups=team, tiled=True)  25.3 us
    ppermute x4, starting transfers between devices, shards(): mine.append(lax.ppermute(block, axes, pairs))  17.2 us
    ppermute x4, starting transfers between devices, share(): return [lax.ppermute(block, axes, across) for block in blocks]  8.78 us
    pallas_call x1, Pallas kernels, shards(): pl.pallas_call(functools.partial(adjoint_kernel, counts, lanes, reach, st...  8.5 us
    ppermute x4, waiting for transfers between devices, share(): return [lax.ppermute(block, axes, across) for block in blocks]  6.72 us
    pallas_call x1, Pallas kernels, run(): pl.pallas_call(functools.partial(forward_kernel, reach, steps, planes, ro...  6.36 us
    all_to_all x1, starting transfers between devices, shards(): lax.all_to_all(grads, axes, 0, 0, axis_index_groups=pair, tiled=True)  6.2 us
    ppermute x1, starting transfers between devices, shards(): mine = [lax.ppermute(block, axes, swap)]  6.03 us
  transfers between devices with their start and end apart: 12, of which 5 were waited for; matrix products, arithmetic and copies ran while one was open for 1% of the time, Pallas kernels for 7%

profile of v4, /device:TPU:1, one launch (start us, length us, event | category | flops | bytes accessed | tf_op | source)
XLA Modules:
  0.0 101.6 jit_solution(566493190313657212)
XLA Ops:
  1.3 2.0 %pack.1 = f32[1360,128]{1,0:T(8,128)} custom-call(s32[1]{0:T(128)S(6)} %copy.25.cell_ref, f32[9,2,32,128]{3,2,1,0:T(8,128)} %bitcast.17, f32[9,2,32,128]{3,2,1,0:T(8,128)} %bitcast.18, f32[2,32,128]{2,1,0:T(8,128)} %lam_ref.1, f32[2,32,128]{2,1,0:T(8,128)} %mu_ref.1, f32[2,32,128]{2,1,0:T(8,128)} %buo_ref.1, f32[8,128]{1,0:T(8,128)} %bitcast.21, ...), custom_call_target="tpu_custom_call" | custom-call | tf_op jit(solution)/shard_map/pack/pallas_call | solution.py:359
  3.3 6.0 %collective-permute-start.4 = (f32[1360,128]{1,0:T(8,128)}, f32[1360,128]{1,0:T(8,128)S(1)}, u32[]{:S(2)}, u32[]{:S(2)}) collective-permute-start(f32[1360,128]{1,0:T(8,128)} %pack.1), channel_id=1, source_target_pairs={{0,0},{1,128},{2,2},{3,130},{4,4},{5,132},{6,6},{7,134},{8,8},{9,1... | collective-permute-start | bytes 2088968 | tf_op jit(solution)/shard_map/ppermute | solution.py:377
  9.3 1.3 %collective-permute-start.5 = (f32[1360,128]{1,0:T(8,128)}, f32[1360,128]{1,0:T(8,128)S(1)}, u32[]{:S(2)}, u32[]{:S(2)}) collective-permute-start(f32[1360,128]{1,0:T(8,128)} %pack.1), channel_id=1, source_target_pairs={{2,128},{1,2},{4,130},{3,4},{6,132},{5,6},{8,134},{7,8},{10,136},{... | collective-permute-start | bytes 2088968 | tf_op jit(solution)/shard_map/ppermute | solution.py:384
  10.6 4.9 %collective-permute-start.6 = (f32[1360,128]{1,0:T(8,128)}, f32[1360,128]{1,0:T(8,128)S(1)}, u32[]{:S(2)}, u32[]{:S(2)}) collective-permute-start(f32[1360,128]{1,0:T(8,128)} %pack.1), channel_id=1, source_target_pairs={{3,128},{0,2},{5,130},{2,4},{7,132},{4,6},{9,134},{6,8},{11,136},{... | collective-permute-start | bytes 2088968 | tf_op jit(solution)/shard_map/ppermute | solution.py:384
  15.5 1.3 %collective-permute-start.7 = (f32[1360,128]{1,0:T(8,128)}, f32[1360,128]{1,0:T(8,128)}, u32[]{:S(2)}, u32[]{:S(2)}) collective-permute-start(f32[1360,128]{1,0:T(8,128)} %pack.1), channel_id=1, source_target_pairs={{4,128},{6,130},{1,4},{8,132},{3,6},{10,134},{5,8},{12,136},{7,10}... | collective-permute-start | bytes 2088968 | tf_op jit(solution)/shard_map/ppermute | solution.py:384
  16.8 9.7 %collective-permute-start.8 = (f32[1360,128]{1,0:T(8,128)}, f32[1360,128]{1,0:T(8,128)}, u32[]{:S(2)}, u32[]{:S(2)}) collective-permute-start(f32[1360,128]{1,0:T(8,128)} %pack.1), channel_id=1, source_target_pairs={{5,128},{7,130},{0,4},{9,132},{2,6},{11,134},{4,8},{13,136},{6,10}... | collective-permute-start | bytes 2088968 | tf_op jit(solution)/shard_map/ppermute | solution.py:384
  26.6 1.0 %letters.1 = f32[128,128]{1,0:T(8,128)} custom-call(f32[1360,128]{1,0:T(8,128)S(1)} %collective-permute-done.4.note_ref.refs_0_), custom_call_target="tpu_custom_call" | custom-call | tf_op jit(solution)/shard_map/letters/pallas_call | solution.py:386
  27.6 25.3 %all-to-all-start = ((f32[128,1,128]{2,1,0:T(1,128)}), f32[128,1,128]{2,1,0:T(1,128)S(1)}, u32[]{:S(2)}, u32[]{:S(2)}) async-start(f32[128,1,128]{2,1,0:T(1,128)} %bitcast.20), calls=%async_computation | async-start | bytes 131072 | tf_op jit(solution)/shard_map/all_to_all | solution.py:395
  53.0 7.0 %conditional.4 = (f32[1360,128]{1,0:T(8,128)}, f32[1360,128]{1,0:T(8,128)}) conditional(s32[]{:T(128)} %convert_element_type.2, (f32[1360,128]{1,0:T(8,128)S(1)}, f32[1360,128]{1,0:T(8,128)S(1)}) %tuple.33, (f32[1360,128]{1,0:T(8,128)S(1)}, f32[1360,128]{1,0:T(8,128)S(1)}) %tuple.33), branch_computations={%region_0.0_spmd, %region_1.0_spmd} | conditional | bytes 5570656 | solution.py:408
  53.0 2.8 %collective-permute-start = (f32[1360,128]{1,0:T(8,128)S(1)}, f32[1360,128]{1,0:T(8,128)}, u32[]{:S(2)}, u32[]{:S(2)}) collective-permute-start(f32[1360,128]{1,0:T(8,128)S(1)} %get-tuple-element.41), channel_id=1, source_target_pairs={{0,128},{128,0},{2,130},{130,2},{4,132},{132,4},{6,134},{134,6},{8... | collective-permute-start | bytes 2088968 | tf_op jit(solution)/shard_map/cond/branch_1_fun/ppermute | solution.py:404
  55.8 1.9 %collective-permute-start.1 = (f32[1360,128]{1,0:T(8,128)S(1)}, f32[1360,128]{1,0:T(8,128)}, u32[]{:S(2)}, u32[]{:S(2)}) collective-permute-start(f32[1360,128]{1,0:T(8,128)S(1)} %get-tuple-element.42), channel_id=1, source_target_pairs={{0,128},{128,0},{2,130},{130,2},{4,132},{132,4},{6,134},{134,6},{8... | collective-permute-start | bytes 2088968 | tf_op jit(solution)/shard_map/cond/branch_1_fun/ppermute | solution.py:404
  57.7 2.2 %collective-permute-done.1 = f32[1360,128]{1,0:T(8,128)} collective-permute-done((f32[1360,128]{1,0:T(8,128)S(1)}, f32[1360,128]{1,0:T(8,128)}, u32[]{:S(2)}, u32[]{:S(2)}) %collective-permute-start.1) | collective-permute-done | bytes 696352 | tf_op jit(solution)/shard_map/cond/branch_1_fun/ppermute | solution.py:404
  60.0 4.2 %conditional.5 = (f32[1360,128]{1,0:T(8,128)}) conditional(s32[]{:T(128)} %convert_element_type.2, f32[1360,128]{1,0:T(8,128)S(1)} %collective-permute-done.6.refs_2_, f32[1360,128]{1,0:T(8,128)S(1)} %collective-permute-done.6.refs_2_), branch_computations={%region_2.0_spmd, %region_3.0_spmd} | conditional | bytes 2785328 | solution.py:409
  60.0 2.0 %collective-permute-start.2 = (f32[1360,128]{1,0:T(8,128)S(1)}, f32[1360,128]{1,0:T(8,128)}, u32[]{:S(2)}, u32[]{:S(2)}) collective-permute-start(f32[1360,128]{1,0:T(8,128)S(1)} %param.3), channel_id=1, source_target_pairs={{0,128},{128,0},{2,130},{130,2},{4,132},{132,4},{6,134},{134,6},{8... | collective-permute-start | bytes 2088968 | tf_op jit(solution)/shard_map/cond/branch_1_fun/ppermute | solution.py:404
  62.0 2.1 %collective-permute-done.2 = f32[1360,128]{1,0:T(8,128)} collective-permute-done((f32[1360,128]{1,0:T(8,128)S(1)}, f32[1360,128]{1,0:T(8,128)}, u32[]{:S(2)}, u32[]{:S(2)}) %collective-permute-start.2) | collective-permute-done | bytes 696352 | tf_op jit(solution)/shard_map/cond/branch_1_fun/ppermute | solution.py:404
  64.2 4.4 %conditional.6 = (f32[1360,128]{1,0:T(8,128)}) conditional(s32[]{:T(128)} %convert_element_type.2, f32[1360,128]{1,0:T(8,128)} %collective-permute-done.7.refs_3_, f32[1360,128]{1,0:T(8,128)} %collective-permute-done.7.refs_3_), branch_computations={%region_4.0_spmd, %region_5.0_spmd} | conditional | bytes 2785328 | solution.py:410
  64.2 2.0 %collective-permute-start.3 = (f32[1360,128]{1,0:T(8,128)}, f32[1360,128]{1,0:T(8,128)}, u32[]{:S(2)}, u32[]{:S(2)}) collective-permute-start(f32[1360,128]{1,0:T(8,128)} %param.5), channel_id=1, source_target_pairs={{0,128},{128,0},{2,130},{130,2},{4,132},{132,4},{6,134},{134,6},{8... | collective-permute-start | bytes 2088968 | tf_op jit(solution)/shard_map/cond/branch_1_fun/ppermute | solution.py:404
  66.2 2.3 %collective-permute-done.3 = f32[1360,128]{1,0:T(8,128)} collective-permute-done((f32[1360,128]{1,0:T(8,128)}, f32[1360,128]{1,0:T(8,128)}, u32[]{:S(2)}, u32[]{:S(2)}) %collective-permute-start.3) | collective-permute-done | bytes 696352 | tf_op jit(solution)/shard_map/cond/branch_1_fun/ppermute | solution.py:404
  68.6 7.2 %conditional.7 = (f32[8,6,2,32,128]{4,3,2,1,0:T(8,128)S(1)}) conditional(s32[]{:T(128)} %convert_element_type.2, () %tuple.34, (s32[2]{0:T(128)S(1)}, f32[1360,128]{1,0:T(8,128)S(1)}, f32[1360,128]{1,0:T(8,128)S(1)}, f32[1360,128]{1,0:T(8,128)S(1)}, f32[1360,128]{1,0:T(8,128)}, /*index=5*/f32[1360,128]{1,0:T(8,128)}, f32[1360,128]{1,0:T(8,128)}, ...), branch_computations={%region_6.0_spmd, %region_7.0_spmd} | conditional | flops 60000000 | bytes 18785316 | solution.py:425
  69.4 6.4 %forward.1 = f32[8,6,2,32,128]{4,3,2,1,0:T(8,128)S(1)} custom-call(s32[2]{0:T(128)S(1)} %get-tuple-element.43.meta_ref, f32[1360,128]{1,0:T(8,128)S(1)} %get-tuple-element.44.refs_0_, f32[1360,128]{1,0:T(8,128)S(1)} %get-tuple-element.45.refs_1_, f32[1360,128]{1,0:T(8,128)} %copy-done.1, f32[1360,128]{1,0:T(8,128)} %get-tuple-element.47.refs_3_, ...), custom_call_target="tpu_custom_call" | custom-call | flops 60000000 | bytes 16000000 | tf_op jit(solution)/shard_map/cond/branch_1_fun/forward/pallas_call | solution.py:413
  76.4 8.5 %adjoint.1 = (f32[576,128]{1,0:T(8,128)}, f32[8,2,2,8,128]{4,3,2,1,0:T(8,128)}) custom-call(s32[2]{0:T(128)S(1)} %pad_add_fusion.meta_ref, f32[1360,128]{1,0:T(8,128)S(1)} %collective-permute-done.4.note_ref.refs_0_, f32[1360,128]{1,0:T(8,128)S(1)} %collective-permute-done.5.refs_1_, f32[1360,128]{1,0:T(8,128)} %copy-done, ...), custom_call_target="tpu_custom_call" | custom-call | flops 60000000 | bytes 16000000 | tf_op jit(solution)/shard_map/adjoint/pallas_call | solution.py:426
  84.9 6.2 %all-to-all-start.1 = ((f32[8,2,2,8,128]{4,3,2,1,0:T(8,128)}), f32[8,2,2,8,128]{4,3,2,1,0:T(8,128)S(1)}, u32[]{:S(2)}, u32[]{:S(2)}) async-start(f32[8,2,2,8,128]{4,3,2,1,0:T(8,128)} %get-tuple-element.63), calls=%async_computation.1 | async-start | bytes 262144 | tf_op jit(solution)/shard_map/all_to_all | solution.py:444
  91.1 5.0 %collective-permute-start.9 = (f32[576,128]{1,0:T(8,128)}, f32[576,128]{1,0:T(8,128)S(1)}, u32[]{:S(2)}, u32[]{:S(2)}) collective-permute-start(f32[576,128]{1,0:T(8,128)} %get-tuple-element.62), channel_id=1, source_target_pairs={{0,0},{1,128},{2,2},{3,130},{4,4},{5,132},{6,6},{7,134},{8,8},{9,1... | collective-permute-start | bytes 884744 | tf_op jit(solution)/shard_map/ppermute | solution.py:443
  97.0 3.9 %collective-permute-done.9 = f32[576,128]{1,0:T(8,128)S(1)} collective-permute-done((f32[576,128]{1,0:T(8,128)}, f32[576,128]{1,0:T(8,128)S(1)}, u32[]{:S(2)}, u32[]{:S(2)}) %collective-permute-start.9) | collective-permute-done | bytes 294944 | tf_op jit(solution)/shard_map/ppermute | solution.py:443
  (18 shorter events, 3.1 us)
Async XLA Ops:
  3.3 23.3 %collective-permute-start.4 = (f32[1360,128]{1,0:T(8,128)}, f32[1360,128]{1,0:T(8,128)S(1)}, u32[]{:S(2)}, u32[]{:S(2)}) collective-permute-start(f32[1360,128]{1,0:T(8,128)} %pack.1), channel_id=1, source_target_pairs={{0,0},{1,128},{2,2},{3,130},{4,4},{5,132},{6,6},{7,134},{8,8},{9,1... | collective-permute-start | bytes 2088968 | tf_op jit(solution)/shard_map/ppermute | solution.py:377
  9.3 43.7 %collective-permute-start.5 = (f32[1360,128]{1,0:T(8,128)}, f32[1360,128]{1,0:T(8,128)S(1)}, u32[]{:S(2)}, u32[]{:S(2)}) collective-permute-start(f32[1360,128]{1,0:T(8,128)} %pack.1), channel_id=1, source_target_pairs={{2,128},{1,2},{4,130},{3,4},{6,132},{5,6},{8,134},{7,8},{10,136},{... | collective-permute-start | bytes 2088968 | tf_op jit(solution)/shard_map/ppermute | solution.py:384
  10.6 49.3 %collective-permute-start.6 = (f32[1360,128]{1,0:T(8,128)}, f32[1360,128]{1,0:T(8,128)S(1)}, u32[]{:S(2)}, u32[]{:S(2)}) collective-permute-start(f32[1360,128]{1,0:T(8,128)} %pack.1), channel_id=1, source_target_pairs={{3,128},{0,2},{5,130},{2,4},{7,132},{4,6},{9,134},{6,8},{11,136},{... | collective-permute-start | bytes 2088968 | tf_op jit(solution)/shard_map/ppermute | solution.py:384
  15.5 48.6 %collective-permute-start.7 = (f32[1360,128]{1,0:T(8,128)}, f32[1360,128]{1,0:T(8,128)}, u32[]{:S(2)}, u32[]{:S(2)}) collective-permute-start(f32[1360,128]{1,0:T(8,128)} %pack.1), channel_id=1, source_target_pairs={{4,128},{6,130},{1,4},{8,132},{3,6},{10,134},{5,8},{12,136},{7,10}... | collective-permute-start | bytes 2088968 | tf_op jit(solution)/shard_map/ppermute | solution.py:384
  16.8 51.7 %collective-permute-start.8 = (f32[1360,128]{1,0:T(8,128)}, f32[1360,128]{1,0:T(8,128)}, u32[]{:S(2)}, u32[]{:S(2)}) collective-permute-start(f32[1360,128]{1,0:T(8,128)} %pack.1), channel_id=1, source_target_pairs={{5,128},{7,130},{0,4},{9,132},{2,6},{11,134},{4,8},{13,136},{6,10}... | collective-permute-start | bytes 2088968 | tf_op jit(solution)/shard_map/ppermute | solution.py:384
  27.6 48.1 %all-to-all-start = ((f32[128,1,128]{2,1,0:T(1,128)}), f32[128,1,128]{2,1,0:T(1,128)S(1)}, u32[]{:S(2)}, u32[]{:S(2)}) async-start(f32[128,1,128]{2,1,0:T(1,128)} %bitcast.20), calls=%async_computation | async-start | bytes 131072 | tf_op jit(solution)/shard_map/all_to_all | solution.py:395
  53.0 4.7 %collective-permute-start = (f32[1360,128]{1,0:T(8,128)S(1)}, f32[1360,128]{1,0:T(8,128)}, u32[]{:S(2)}, u32[]{:S(2)}) collective-permute-start(f32[1360,128]{1,0:T(8,128)S(1)} %get-tuple-element.41), channel_id=1, source_target_pairs={{0,128},{128,0},{2,130},{130,2},{4,132},{132,4},{6,134},{134,6},{8... | collective-permute-start | bytes 2088968 | tf_op jit(solution)/shard_map/cond/branch_1_fun/ppermute | solution.py:404
  55.8 4.2 %collective-permute-start.1 = (f32[1360,128]{1,0:T(8,128)S(1)}, f32[1360,128]{1,0:T(8,128)}, u32[]{:S(2)}, u32[]{:S(2)}) collective-permute-start(f32[1360,128]{1,0:T(8,128)S(1)} %get-tuple-element.42), channel_id=1, source_target_pairs={{0,128},{128,0},{2,130},{130,2},{4,132},{132,4},{6,134},{134,6},{8... | collective-permute-start | bytes 2088968 | tf_op jit(solution)/shard_map/cond/branch_1_fun/ppermute | solution.py:404
  60.0 8.6 %copy-start = (f32[1360,128]{1,0:T(8,128)}, f32[1360,128]{1,0:T(8,128)S(1)}, u32[]{:S(2)}) copy-start(f32[1360,128]{1,0:T(8,128)S(1)} %collective-permute-done.6.refs_2_) | copy-start | bytes 2088964
  60.0 4.2 %collective-permute-start.2 = (f32[1360,128]{1,0:T(8,128)S(1)}, f32[1360,128]{1,0:T(8,128)}, u32[]{:S(2)}, u32[]{:S(2)}) collective-permute-start(f32[1360,128]{1,0:T(8,128)S(1)} %param.3), channel_id=1, source_target_pairs={{0,128},{128,0},{2,130},{130,2},{4,132},{132,4},{6,134},{134,6},{8... | collective-permute-start | bytes 2088968 | tf_op jit(solution)/shard_map/cond/branch_1_fun/ppermute | solution.py:404
  64.2 4.4 %collective-permute-start.3 = (f32[1360,128]{1,0:T(8,128)}, f32[1360,128]{1,0:T(8,128)}, u32[]{:S(2)}, u32[]{:S(2)}) collective-permute-start(f32[1360,128]{1,0:T(8,128)} %param.5), channel_id=1, source_target_pairs={{0,128},{128,0},{2,130},{130,2},{4,132},{132,4},{6,134},{134,6},{8... | collective-permute-start | bytes 2088968 | tf_op jit(solution)/shard_map/cond/branch_1_fun/ppermute | solution.py:404
  68.6 0.9 copy-start.1
  75.8 0.6 copy-start.2
  84.9 11.5 %all-to-all-start.1 = ((f32[8,2,2,8,128]{4,3,2,1,0:T(8,128)}), f32[8,2,2,8,128]{4,3,2,1,0:T(8,128)S(1)}, u32[]{:S(2)}, u32[]{:S(2)}) async-start(f32[8,2,2,8,128]{4,3,2,1,0:T(8,128)} %get-tuple-element.63), calls=%async_computation.1 | async-start | bytes 262144 | tf_op jit(solution)/shard_map/all_to_all | solution.py:444
  91.1 9.7 %collective-permute-start.9 = (f32[576,128]{1,0:T(8,128)}, f32[576,128]{1,0:T(8,128)S(1)}, u32[]{:S(2)}, u32[]{:S(2)}) collective-permute-start(f32[576,128]{1,0:T(8,128)} %get-tuple-element.62), channel_id=1, source_target_pairs={{0,0},{1,128},{2,2},{3,130},{4,4},{5,132},{6,6},{7,134},{8,8},{9,1... | collective-permute-start | bytes 884744 | tf_op jit(solution)/shard_map/ppermute | solution.py:443

commit v5 on v4

--- a/solution.py
+++ b/solution.py
@@ -100,7 +100,7 @@
     out_ref[at + steps : at + steps + 1] = slab_ref[...].astype(jnp.float32)
     out_ref[at + steps + 1 : at + steps + 2] = spot_ref[...].astype(jnp.float32)
     out_ref[at + steps + 2 : at + steps + 3, 0:steps] = wave_ref[...]
-    out_ref[at + steps + 3 : at + steps + 4] = jnp.full((1, depth), cell_ref[0], jnp.int32).astype(jnp.float32)
+    out_ref[at + steps + 3 : at + steps + 4] = jnp.broadcast_to(cell_ref[...], (1, depth)).astype(jnp.float32)
 
 
 class Window:
@@ -359,11 +359,11 @@
     block = pl.pallas_call(
         pack_kernel,
         out_shape=jax.ShapeDtypeStruct((height, depth), jnp.float32),
-        in_specs=[smem()] + [vmem()] * 9,
+        in_specs=[vmem()] * 10,
         out_specs=vmem(),
         name="pack",
     )(
-        source_cell,
+        source_cell.reshape(1, 1),
         forward_state[0],
         adjoint_state[0],
         lame_lambda,

time: 103 us -> 103 us (level)
  no operation moved by 1% of the time
where the time goes in v5:
time: 103 us; the launch traced here: 102 us
  starting transfers between devices  69.1 us (67%)
  Pallas kernels  18 us (17%)
  waiting for transfers between devices  10.8 us (10%)
  local copies, waits for them, and re-layouts  2.81 us (3%)
  between operations  1.39 us (1%)
    all_to_all x1, starting transfers between devices, shards(): lax.all_to_all(letters, axes, 0, 0, axis_index_groups=team, tiled=True)  25.3 us
    ppermute x4, starting transfers between devices, shards(): mine.append(lax.ppermute(block, axes, pairs))  17.2 us
    ppermute x4, starting transfers between devices, share(): return [lax.ppermute(block, axes, across) for block in blocks]  8.78 us
    pallas_call x1, Pallas kernels, shards(): pl.pallas_call(functools.partial(adjoint_kernel, counts, lanes, reach, st...  8.5 us
    all_to_all x1, starting transfers between devices, shards(): lax.all_to_all(grads, axes, 0, 0, axis_index_groups=pair, tiled=True)  6.77 us
    ppermute x4, waiting for transfers between devices, share(): return [lax.ppermute(block, axes, across) for block in blocks]  6.72 us
    pallas_call x1, Pallas kernels, run(): pl.pallas_call(functools.partial(forward_kernel, reach, steps, planes, ro...  6.36 us
    ppermute x1, starting transfers between devices, shards(): mine = [lax.ppermute(block, axes, swap)]  6.03 us
  transfers between devices with their start and end apart: 12, of which 5 were waited for; matrix products, arithmetic and copies ran while one was open for 1% of the time, Pallas kernels for 7%

profile of v5, /device:TPU:1, one launch (start us, length us, event | category | flops | bytes accessed | tf_op | source)
XLA Modules:
  0.0 102.2 jit_solution(1732341654818201361)
XLA Ops:
  1.3 2.0 %pack.1 = f32[1360,128]{1,0:T(8,128)} custom-call(s32[1,1]{1,0:T(1,128)} %bitcast.17.cell_ref, f32[9,2,32,128]{3,2,1,0:T(8,128)} %bitcast.19, f32[9,2,32,128]{3,2,1,0:T(8,128)} %bitcast.20, f32[2,32,128]{2,1,0:T(8,128)} %lam_ref.1, f32[2,32,128]{2,1,0:T(8,128)} %mu_ref.1, f32[2,32,128]{2,1,0:T(8,128)} %buo_ref.1, f32[8,128]{1,0:T(8,128)} %bitcast.23, ...), custom_call_target="tpu_custom_call" | custom-call | tf_op jit(solution)/shard_map/pack/pallas_call | solution.py:359
  3.3 6.0 %collective-permute-start.4 = (f32[1360,128]{1,0:T(8,128)}, f32[1360,128]{1,0:T(8,128)S(1)}, u32[]{:S(2)}, u32[]{:S(2)}) collective-permute-start(f32[1360,128]{1,0:T(8,128)} %pack.1), channel_id=1, source_target_pairs={{0,0},{1,128},{2,2},{3,130},{4,4},{5,132},{6,6},{7,134},{8,8},{9,1... | collective-permute-start | bytes 2088968 | tf_op jit(solution)/shard_map/ppermute | solution.py:377
  9.4 1.3 %collective-permute-start.5 = (f32[1360,128]{1,0:T(8,128)}, f32[1360,128]{1,0:T(8,128)S(1)}, u32[]{:S(2)}, u32[]{:S(2)}) collective-permute-start(f32[1360,128]{1,0:T(8,128)} %pack.1), channel_id=1, source_target_pairs={{2,128},{1,2},{4,130},{3,4},{6,132},{5,6},{8,134},{7,8},{10,136},{... | collective-permute-start | bytes 2088968 | tf_op jit(solution)/shard_map/ppermute | solution.py:384
  10.7 4.9 %collective-permute-start.6 = (f32[1360,128]{1,0:T(8,128)}, f32[1360,128]{1,0:T(8,128)S(1)}, u32[]{:S(2)}, u32[]{:S(2)}) collective-permute-start(f32[1360,128]{1,0:T(8,128)} %pack.1), channel_id=1, source_target_pairs={{3,128},{0,2},{5,130},{2,4},{7,132},{4,6},{9,134},{6,8},{11,136},{... | collective-permute-start | bytes 2088968 | tf_op jit(solution)/shard_map/ppermute | solution.py:384
  15.6 1.3 %collective-permute-start.7 = (f32[1360,128]{1,0:T(8,128)}, f32[1360,128]{1,0:T(8,128)}, u32[]{:S(2)}, u32[]{:S(2)}) collective-permute-start(f32[1360,128]{1,0:T(8,128)} %pack.1), channel_id=1, source_target_pairs={{4,128},{6,130},{1,4},{8,132},{3,6},{10,134},{5,8},{12,136},{7,10}... | collective-permute-start | bytes 2088968 | tf_op jit(solution)/shard_map/ppermute | solution.py:384
  16.9 9.7 %collective-permute-start.8 = (f32[1360,128]{1,0:T(8,128)}, f32[1360,128]{1,0:T(8,128)}, u32[]{:S(2)}, u32[]{:S(2)}) collective-permute-start(f32[1360,128]{1,0:T(8,128)} %pack.1), channel_id=1, source_target_pairs={{5,128},{7,130},{0,4},{9,132},{2,6},{11,134},{4,8},{13,136},{6,10}... | collective-permute-start | bytes 2088968 | tf_op jit(solution)/shard_map/ppermute | solution.py:384
  26.6 1.0 %letters.1 = f32[128,128]{1,0:T(8,128)} custom-call(f32[1360,128]{1,0:T(8,128)S(1)} %collective-permute-done.4.note_ref.refs_0_), custom_call_target="tpu_custom_call" | custom-call | tf_op jit(solution)/shard_map/letters/pallas_call | solution.py:386
  27.7 25.3 %all-to-all-start = ((f32[128,1,128]{2,1,0:T(1,128)}), f32[128,1,128]{2,1,0:T(1,128)S(1)}, u32[]{:S(2)}, u32[]{:S(2)}) async-start(f32[128,1,128]{2,1,0:T(1,128)} %bitcast.22), calls=%async_computation | async-start | bytes 131072 | tf_op jit(solution)/shard_map/all_to_all | solution.py:395
  53.0 7.0 %conditional.4 = (f32[1360,128]{1,0:T(8,128)}, f32[1360,128]{1,0:T(8,128)}) conditional(s32[]{:T(128)} %convert_element_type.2, (f32[1360,128]{1,0:T(8,128)S(1)}, f32[1360,128]{1,0:T(8,128)S(1)}) %tuple.33, (f32[1360,128]{1,0:T(8,128)S(1)}, f32[1360,128]{1,0:T(8,128)S(1)}) %tuple.33), branch_computations={%region_0.0_spmd, %region_1.0_spmd} | conditional | bytes 5570656 | solution.py:408
  53.0 2.8 %collective-permute-start = (f32[1360,128]{1,0:T(8,128)S(1)}, f32[1360,128]{1,0:T(8,128)}, u32[]{:S(2)}, u32[]{:S(2)}) collective-permute-start(f32[1360,128]{1,0:T(8,128)S(1)} %get-tuple-element.41), channel_id=1, source_target_pairs={{0,128},{128,0},{2,130},{130,2},{4,132},{132,4},{6,134},{134,6},{8... | collective-permute-start | bytes 2088968 | tf_op jit(solution)/shard_map/cond/branch_1_fun/ppermute | solution.py:404
  55.8 1.9 %collective-permute-start.1 = (f32[1360,128]{1,0:T(8,128)S(1)}, f32[1360,128]{1,0:T(8,128)}, u32[]{:S(2)}, u32[]{:S(2)}) collective-permute-start(f32[1360,128]{1,0:T(8,128)S(1)} %get-tuple-element.42), channel_id=1, source_target_pairs={{0,128},{128,0},{2,130},{130,2},{4,132},{132,4},{6,134},{134,6},{8... | collective-permute-start | bytes 2088968 | tf_op jit(solution)/shard_map/cond/branch_1_fun/ppermute | solution.py:404
  57.8 2.2 %collective-permute-done.1 = f32[1360,128]{1,0:T(8,128)} collective-permute-done((f32[1360,128]{1,0:T(8,128)S(1)}, f32[1360,128]{1,0:T(8,128)}, u32[]{:S(2)}, u32[]{:S(2)}) %collective-permute-start.1) | collective-permute-done | bytes 696352 | tf_op jit(solution)/shard_map/cond/branch_1_fun/ppermute | solution.py:404
  60.0 4.2 %conditional.5 = (f32[1360,128]{1,0:T(8,128)}) conditional(s32[]{:T(128)} %convert_element_type.2, f32[1360,128]{1,0:T(8,128)S(1)} %collective-permute-done.6.refs_2_, f32[1360,128]{1,0:T(8,128)S(1)} %collective-permute-done.6.refs_2_), branch_computations={%region_2.0_spmd, %region_3.0_spmd} | conditional | bytes 2785328 | solution.py:409
  60.0 2.0 %collective-permute-start.2 = (f32[1360,128]{1,0:T(8,128)S(1)}, f32[1360,128]{1,0:T(8,128)}, u32[]{:S(2)}, u32[]{:S(2)}) collective-permute-start(f32[1360,128]{1,0:T(8,128)S(1)} %param.3), channel_id=1, source_target_pairs={{0,128},{128,0},{2,130},{130,2},{4,132},{132,4},{6,134},{134,6},{8... | collective-permute-start | bytes 2088968 | tf_op jit(solution)/shard_map/cond/branch_1_fun/ppermute | solution.py:404
  62.1 2.1 %collective-permute-done.2 = f32[1360,128]{1,0:T(8,128)} collective-permute-done((f32[1360,128]{1,0:T(8,128)S(1)}, f32[1360,128]{1,0:T(8,128)}, u32[]{:S(2)}, u32[]{:S(2)}) %collective-permute-start.2) | collective-permute-done | bytes 696352 | tf_op jit(solution)/shard_map/cond/branch_1_fun/ppermute | solution.py:404
  64.2 4.4 %conditional.6 = (f32[1360,128]{1,0:T(8,128)}) conditional(s32[]{:T(128)} %convert_element_type.2, f32[1360,128]{1,0:T(8,128)} %collective-permute-done.7.refs_3_, f32[1360,128]{1,0:T(8,128)} %collective-permute-done.7.refs_3_), branch_computations={%region_4.0_spmd, %region_5.0_spmd} | conditional | bytes 2785328 | solution.py:410
  64.2 2.0 %collective-permute-start.3 = (f32[1360,128]{1,0:T(8,128)}, f32[1360,128]{1,0:T(8,128)}, u32[]{:S(2)}, u32[]{:S(2)}) collective-permute-start(f32[1360,128]{1,0:T(8,128)} %param.5), channel_id=1, source_target_pairs={{0,128},{128,0},{2,130},{130,2},{4,132},{132,4},{6,134},{134,6},{8... | collective-permute-start | bytes 2088968 | tf_op jit(solution)/shard_map/cond/branch_1_fun/ppermute | solution.py:404
  66.2 2.3 %collective-permute-done.3 = f32[1360,128]{1,0:T(8,128)} collective-permute-done((f32[1360,128]{1,0:T(8,128)}, f32[1360,128]{1,0:T(8,128)}, u32[]{:S(2)}, u32[]{:S(2)}) %collective-permute-start.3) | collective-permute-done | bytes 696352 | tf_op jit(solution)/shard_map/cond/branch_1_fun/ppermute | solution.py:404
  68.6 7.2 %conditional.7 = (f32[8,6,2,32,128]{4,3,2,1,0:T(8,128)S(1)}) conditional(s32[]{:T(128)} %convert_element_type.2, () %tuple.34, (s32[2]{0:T(128)S(1)}, f32[1360,128]{1,0:T(8,128)S(1)}, f32[1360,128]{1,0:T(8,128)S(1)}, f32[1360,128]{1,0:T(8,128)S(1)}, f32[1360,128]{1,0:T(8,128)}, /*index=5*/f32[1360,128]{1,0:T(8,128)}, f32[1360,128]{1,0:T(8,128)}, ...), branch_computations={%region_6.0_spmd, %region_7.0_spmd} | conditional | flops 60000000 | bytes 18785316 | solution.py:425
  69.4 6.4 %forward.1 = f32[8,6,2,32,128]{4,3,2,1,0:T(8,128)S(1)} custom-call(s32[2]{0:T(128)S(1)} %get-tuple-element.43.meta_ref, f32[1360,128]{1,0:T(8,128)S(1)} %get-tuple-element.44.refs_0_, f32[1360,128]{1,0:T(8,128)S(1)} %get-tuple-element.45.refs_1_, f32[1360,128]{1,0:T(8,128)} %copy-done.1, f32[1360,128]{1,0:T(8,128)} %get-tuple-element.47.refs_3_, ...), custom_call_target="tpu_custom_call" | custom-call | flops 60000000 | bytes 16000000 | tf_op jit(solution)/shard_map/cond/branch_1_fun/forward/pallas_call | solution.py:413
  76.5 8.5 %adjoint.1 = (f32[576,128]{1,0:T(8,128)}, f32[8,2,2,8,128]{4,3,2,1,0:T(8,128)}) custom-call(s32[2]{0:T(128)S(1)} %pad_add_fusion.meta_ref, f32[1360,128]{1,0:T(8,128)S(1)} %collective-permute-done.4.note_ref.refs_0_, f32[1360,128]{1,0:T(8,128)S(1)} %collective-permute-done.5.refs_1_, f32[1360,128]{1,0:T(8,128)} %copy-done, ...), custom_call_target="tpu_custom_call" | custom-call | flops 60000000 | bytes 16000000 | tf_op jit(solution)/shard_map/adjoint/pallas_call | solution.py:426
  85.0 6.8 %all-to-all-start.1 = ((f32[8,2,2,8,128]{4,3,2,1,0:T(8,128)}), f32[8,2,2,8,128]{4,3,2,1,0:T(8,128)S(1)}, u32[]{:S(2)}, u32[]{:S(2)}) async-start(f32[8,2,2,8,128]{4,3,2,1,0:T(8,128)} %get-tuple-element.63), calls=%async_computation.1 | async-start | bytes 262144 | tf_op jit(solution)/shard_map/all_to_all | solution.py:444
  91.7 5.0 %collective-permute-start.9 = (f32[576,128]{1,0:T(8,128)}, f32[576,128]{1,0:T(8,128)S(1)}, u32[]{:S(2)}, u32[]{:S(2)}) collective-permute-start(f32[576,128]{1,0:T(8,128)} %get-tuple-element.62), channel_id=1, source_target_pairs={{0,0},{1,128},{2,2},{3,130},{4,4},{5,132},{6,6},{7,134},{8,8},{9,1... | collective-permute-start | bytes 884744 | tf_op jit(solution)/shard_map/ppermute | solution.py:443
  97.6 3.9 %collective-permute-done.9 = f32[576,128]{1,0:T(8,128)S(1)} collective-permute-done((f32[576,128]{1,0:T(8,128)}, f32[576,128]{1,0:T(8,128)S(1)}, u32[]{:S(2)}, u32[]{:S(2)}) %collective-permute-start.9) | collective-permute-done | bytes 294944 | tf_op jit(solution)/shard_map/ppermute | solution.py:443
  (18 shorter events, 3.1 us)
Async XLA Ops:
  3.3 23.3 %collective-permute-start.4 = (f32[1360,128]{1,0:T(8,128)}, f32[1360,128]{1,0:T(8,128)S(1)}, u32[]{:S(2)}, u32[]{:S(2)}) collective-permute-start(f32[1360,128]{1,0:T(8,128)} %pack.1), channel_id=1, source_target_pairs={{0,0},{1,128},{2,2},{3,130},{4,4},{5,132},{6,6},{7,134},{8,8},{9,1... | collective-permute-start | bytes 2088968 | tf_op jit(solution)/shard_map/ppermute | solution.py:377
  9.4 43.7 %collective-permute-start.5 = (f32[1360,128]{1,0:T(8,128)}, f32[1360,128]{1,0:T(8,128)S(1)}, u32[]{:S(2)}, u32[]{:S(2)}) collective-permute-start(f32[1360,128]{1,0:T(8,128)} %pack.1), channel_id=1, source_target_pairs={{2,128},{1,2},{4,130},{3,4},{6,132},{5,6},{8,134},{7,8},{10,136},{... | collective-permute-start | bytes 2088968 | tf_op jit(solution)/shard_map/ppermute | solution.py:384
  10.7 49.3 %collective-permute-start.6 = (f32[1360,128]{1,0:T(8,128)}, f32[1360,128]{1,0:T(8,128)S(1)}, u32[]{:S(2)}, u32[]{:S(2)}) collective-permute-start(f32[1360,128]{1,0:T(8,128)} %pack.1), channel_id=1, source_target_pairs={{3,128},{0,2},{5,130},{2,4},{7,132},{4,6},{9,134},{6,8},{11,136},{... | collective-permute-start | bytes 2088968 | tf_op jit(solution)/shard_map/ppermute | solution.py:384
  15.6 48.6 %collective-permute-start.7 = (f32[1360,128]{1,0:T(8,128)}, f32[1360,128]{1,0:T(8,128)}, u32[]{:S(2)}, u32[]{:S(2)}) collective-permute-start(f32[1360,128]{1,0:T(8,128)} %pack.1), channel_id=1, source_target_pairs={{4,128},{6,130},{1,4},{8,132},{3,6},{10,134},{5,8},{12,136},{7,10}... | collective-permute-start | bytes 2088968 | tf_op jit(solution)/shard_map/ppermute | solution.py:384
  16.9 51.7 %collective-permute-start.8 = (f32[1360,128]{1,0:T(8,128)}, f32[1360,128]{1,0:T(8,128)}, u32[]{:S(2)}, u32[]{:S(2)}) collective-permute-start(f32[1360,128]{1,0:T(8,128)} %pack.1), channel_id=1, source_target_pairs={{5,128},{7,130},{0,4},{9,132},{2,6},{11,134},{4,8},{13,136},{6,10}... | collective-permute-start | bytes 2088968 | tf_op jit(solution)/shard_map/ppermute | solution.py:384
  27.7 48.1 %all-to-all-start = ((f32[128,1,128]{2,1,0:T(1,128)}), f32[128,1,128]{2,1,0:T(1,128)S(1)}, u32[]{:S(2)}, u32[]{:S(2)}) async-start(f32[128,1,128]{2,1,0:T(1,128)} %bitcast.22), calls=%async_computation | async-start | bytes 131072 | tf_op jit(solution)/shard_map/all_to_all | solution.py:395
  53.0 4.7 %collective-permute-start = (f32[1360,128]{1,0:T(8,128)S(1)}, f32[1360,128]{1,0:T(8,128)}, u32[]{:S(2)}, u32[]{:S(2)}) collective-permute-start(f32[1360,128]{1,0:T(8,128)S(1)} %get-tuple-element.41), channel_id=1, source_target_pairs={{0,128},{128,0},{2,130},{130,2},{4,132},{132,4},{6,134},{134,6},{8... | collective-permute-start | bytes 2088968 | tf_op jit(solution)/shard_map/cond/branch_1_fun/ppermute | solution.py:404
  55.8 4.2 %collective-permute-start.1 = (f32[1360,128]{1,0:T(8,128)S(1)}, f32[1360,128]{1,0:T(8,128)}, u32[]{:S(2)}, u32[]{:S(2)}) collective-permute-start(f32[1360,128]{1,0:T(8,128)S(1)} %get-tuple-element.42), channel_id=1, source_target_pairs={{0,128},{128,0},{2,130},{130,2},{4,132},{132,4},{6,134},{134,6},{8... | collective-permute-start | bytes 2088968 | tf_op jit(solution)/shard_map/cond/branch_1_fun/ppermute | solution.py:404
  60.0 8.6 %copy-start = (f32[1360,128]{1,0:T(8,128)}, f32[1360,128]{1,0:T(8,128)S(1)}, u32[]{:S(2)}) copy-start(f32[1360,128]{1,0:T(8,128)S(1)} %collective-permute-done.6.refs_2_) | copy-start | bytes 2088964
  60.0 4.2 %collective-permute-start.2 = (f32[1360,128]{1,0:T(8,128)S(1)}, f32[1360,128]{1,0:T(8,128)}, u32[]{:S(2)}, u32[]{:S(2)}) collective-permute-start(f32[1360,128]{1,0:T(8,128)S(1)} %param.3), channel_id=1, source_target_pairs={{0,128},{128,0},{2,130},{130,2},{4,132},{132,4},{6,134},{134,6},{8... | collective-permute-start | bytes 2088968 | tf_op jit(solution)/shard_map/cond/branch_1_fun/ppermute | solution.py:404
  64.2 4.4 %collective-permute-start.3 = (f32[1360,128]{1,0:T(8,128)}, f32[1360,128]{1,0:T(8,128)}, u32[]{:S(2)}, u32[]{:S(2)}) collective-permute-start(f32[1360,128]{1,0:T(8,128)} %param.5), channel_id=1, source_target_pairs={{0,128},{128,0},{2,130},{130,2},{4,132},{132,4},{6,134},{134,6},{8... | collective-permute-start | bytes 2088968 | tf_op jit(solution)/shard_map/cond/branch_1_fun/ppermute | solution.py:404
  68.6 0.9 copy-start.1
  75.8 0.6 copy-start.2
  85.0 12.0 %all-to-all-start.1 = ((f32[8,2,2,8,128]{4,3,2,1,0:T(8,128)}), f32[8,2,2,8,128]{4,3,2,1,0:T(8,128)S(1)}, u32[]{:S(2)}, u32[]{:S(2)}) async-start(f32[8,2,2,8,128]{4,3,2,1,0:T(8,128)} %get-tuple-element.63), calls=%async_computation.1 | async-start | bytes 262144 | tf_op jit(solution)/shard_map/all_to_all | solution.py:444
  91.7 9.7 %collective-permute-start.9 = (f32[576,128]{1,0:T(8,128)}, f32[576,128]{1,0:T(8,128)S(1)}, u32[]{:S(2)}, u32[]{:S(2)}) collective-permute-start(f32[576,128]{1,0:T(8,128)} %get-tuple-element.62), channel_id=1, source_target_pairs={{0,0},{1,128},{2,2},{3,130},{4,4},{5,132},{6,6},{7,134},{8,8},{9,1... | collective-permute-start | bytes 884744 | tf_op jit(solution)/shard_map/ppermute | solution.py:443
